TPU v7x, 32 devices: a whole 2x2x4 slice. The times are simulated.
32 devices in a mesh: patch: 8 (over z, y), var: 4 (over x, core).
Axes of the slice: x: 2, y: 2, z: 4, core: 2. Of those that a mesh axis runs over, the one named last changes fastest.
Arguments:
- input_field: bfloat16 [4, 1024, 48, 16], P(None, 'patch', 'var'), may hold values from -6 to 6
- counts: int32 [4], replicated, may hold values from 256 to 1024, as said below
- var_ids: int32 [4, 48], replicated, may hold values from 0 to 47, each once within a row
- patch_weight: bfloat16 [48, 16, 1024], replicated, may hold values from -1.5 to 1.5
- var_embed: bfloat16 [48, 1024], replicated, may hold values from -6 to 6
- agg_query: bfloat16 [1024], replicated, may hold values from -6 to 6
- query_proj: bfloat16 [1024, 1024], replicated, may hold values from -0.1875 to 0.1875
- key_proj: bfloat16 [1024, 1024], replicated, may hold values from -0.1875 to 0.1875
- value_proj: bfloat16 [1024, 1024], replicated, may hold values from -0.1875 to 0.1875
- agg_out: bfloat16 [1024, 1024], replicated, may hold values from -0.375 to 0.375
- norm_one: bfloat16 [1024], replicated, may hold values from 0.099609375 to 1.8984375
- trunk_qkv: bfloat16 [1024, 3072], replicated, may hold values from -0.1875 to 0.1875
- trunk_out: bfloat16 [1024, 1024], replicated, may hold values from -1.5 to 1.5
- norm_two: bfloat16 [1024], replicated, may hold values from 0.099609375 to 1.8984375
- mlp_in: bfloat16 [1024, 4096], replicated, may hold values from -0.1875 to 0.1875
- mlp_out: bfloat16 [4096, 1024], replicated, may hold values from -0.09375 to 0.09375
- cotangent: bfloat16 [4, 1024, 1024], P('var', 'patch'), may hold values from -6 to 6
Outputs:
- block_out: bfloat16 [4, 1024, 1024], P('var', 'patch')
- field_grad: bfloat16 [4, 1024, 48, 16], P(None, 'patch', 'var')
- patch_weight_grad: float32 [48, 16, 1024], P(None, None, 'patch')
- var_embed_grad: float32 [48, 1024], P(None, 'patch')
- agg_query_grad: float32 [1024], P('patch')
- query_proj_grad: float32 [1024, 1024], P('patch')
- key_proj_grad: float32 [1024, 1024], P('patch')
- value_proj_grad: float32 [1024, 1024], P('patch')
- agg_out_grad: float32 [1024, 1024], P('patch')
- norm_one_grad: float32 [1024], P('patch')
- trunk_qkv_grad: float32 [1024, 3072], P('patch')
- trunk_out_grad: float32 [1024, 1024], P('patch')
- norm_two_grad: float32 [1024], P('patch')
- mlp_in_grad: float32 [1024, 4096], P('patch')
- mlp_out_grad: float32 [4096, 1024], P('patch')
Inputs may be any that keep to these rules, and one draw needn't show every extreme that they name: Each sample fills its first counts slots; every count is 256 or 1024; some sample has 1024 and some other sample has 256. `var_ids`: each row is a permutation of the 48 variables.
All inputs are finite; a program needn't handle non-finite values.
Results may differ from a plain program's by a relative error of at most 0.04.
Values may be sent and summed in bfloat16 or wider, within the bound.
No kernel may reach another device: no remote copies, remote signals or barrier semaphores. Data moves between devices by JAX's collectives and lax.ppermute only.
A program may use at most 384 MiB of HBM per device.

v0:
```python
import math

import jax
import jax.numpy as jnp
from jax import lax
from jax.sharding import PartitionSpec as P

HEADS = 16
VARS = 48


EPSILON = 1e-05
MASKED = -1e30
HIGHEST = lax.Precision.HIGHEST


def layer_norm(values, gain_vec):
    average = jnp.mean(values, axis=-1, keepdims=True)
    center = values - average
    spread = jnp.mean(center * center, axis=-1, keepdims=True)
    return center * lax.rsqrt(spread + EPSILON) * gain_vec


def gelu_exact(values):
    return jax.nn.gelu(values, approximate=False)


def front_forward(field_part, id_part, patch_weight, var_embed, agg_q, key_proj, value_proj):
    num_rows, seg_len, var_count, pixels = field_part.shape
    model_width = key_proj.shape[0]
    head_dim = model_width // HEADS
    scaling = 1.0 / math.sqrt(head_dim)
    onehot = (id_part[:, :, None] == jnp.arange(VARS, dtype=jnp.int32)[None, None, :]).astype(
        jnp.bfloat16
    )
    sel_weight = jnp.einsum(
        "bjv,vxd->bjxd", onehot, patch_weight, preferred_element_type=jnp.float32
    ).astype(jnp.bfloat16)
    sel_embed = jnp.einsum("bjv,vd->bjd", onehot, var_embed, preferred_element_type=jnp.float32)
    embedded = (
        jnp.einsum("bljx,bjxd->bljd", field_part, sel_weight, preferred_element_type=jnp.float32)
        + sel_embed[:, None]
    ).astype(jnp.bfloat16)
    flat_rows = embedded.reshape(-1, model_width)
    key_rows = jnp.dot(flat_rows, key_proj, preferred_element_type=jnp.float32).astype(jnp.bfloat16)
    value_rows = jnp.dot(flat_rows, value_proj, preferred_element_type=jnp.float32).astype(
        jnp.bfloat16
    )
    shape_heads = (num_rows, seg_len, var_count, HEADS, head_dim)
    scores = (
        jnp.sum(
            key_rows.reshape(shape_heads).astype(jnp.float32) * agg_q.reshape(HEADS, head_dim),
            axis=-1,
        )
        * scaling
    )
    row_max = jnp.max(scores, axis=2)
    exponent = jnp.exp(scores - row_max[:, :, None])
    total_sum = jnp.sum(exponent, axis=2)
    weighted = jnp.einsum(
        "bljh,bljhk->blhk",
        exponent,
        value_rows.reshape(shape_heads),
        preferred_element_type=jnp.float32,
    )
    kept_front = (onehot, sel_weight, embedded, key_rows, value_rows, scores)
    return (row_max, total_sum, weighted, kept_front)


def front_backward(
    field_part, kept_front, mixed_grad, log_total, share_dot, agg_q, key_proj, value_proj
):
    onehot, sel_weight, embedded, key_rows, value_rows, scores = kept_front
    num_rows, seg_len, var_count, pixels = field_part.shape
    model_width = key_proj.shape[0]
    head_dim = model_width // HEADS
    scaling = 1.0 / math.sqrt(head_dim)
    shape_heads = (num_rows, seg_len, var_count, HEADS, head_dim)
    shares = jnp.exp(scores - log_total[:, :, None])
    mixed_heads = mixed_grad.reshape(num_rows, seg_len, 1, HEADS, head_dim).astype(jnp.float32)
    value_grad = (shares[..., None] * mixed_heads).astype(jnp.bfloat16).reshape(-1, model_width)
    share_grad = jnp.sum(value_rows.reshape(shape_heads).astype(jnp.float32) * mixed_heads, axis=-1)
    score_grad = shares * (share_grad - share_dot[:, :, None])
    key_grad = (
        (score_grad[..., None] * (agg_q.reshape(HEADS, head_dim) * scaling))
        .astype(jnp.bfloat16)
        .reshape(-1, model_width)
    )
    query_grad = (
        jnp.einsum(
            "bljh,bljhk->hk",
            score_grad,
            key_rows.reshape(shape_heads),
            preferred_element_type=jnp.float32,
        ).reshape(model_width)
        * scaling
    )
    flat_rows = embedded.reshape(-1, model_width)
    key_proj_grad = jnp.einsum("nd,ne->de", flat_rows, key_grad, preferred_element_type=jnp.float32)
    value_proj_grad = jnp.einsum(
        "nd,ne->de", flat_rows, value_grad, preferred_element_type=jnp.float32
    )
    embed_grad = jnp.einsum(
        "ne,de->nd", key_grad, key_proj, preferred_element_type=jnp.float32
    ) + jnp.einsum("ne,de->nd", value_grad, value_proj, preferred_element_type=jnp.float32)
    embed_grad = embed_grad.astype(jnp.bfloat16).reshape(num_rows, seg_len, var_count, model_width)
    field_grad = jnp.einsum(
        "bljd,bjxd->bljx", embed_grad, sel_weight, preferred_element_type=jnp.float32
    ).astype(jnp.bfloat16)
    sel_grad = jnp.einsum(
        "bljx,bljd->bjxd", field_part, embed_grad, preferred_element_type=jnp.float32
    )
    embed_sum = jnp.sum(embed_grad.astype(jnp.float32), axis=1)
    choose = onehot.astype(jnp.float32)
    patch_grad = jnp.einsum("bjv,bjxd->vxd", choose, sel_grad, precision=HIGHEST)
    vembed_grad = jnp.einsum("bjv,bjd->vd", choose, embed_sum, precision=HIGHEST)
    return (field_grad, patch_grad, vembed_grad, query_grad, key_proj_grad, value_proj_grad)


def local(
    input_field,
    counts,
    var_ids,
    patch_weight,
    var_embed,
    agg_query,
    query_proj,
    key_proj,
    value_proj,
    agg_out,
    norm_one,
    trunk_qkv,
    trunk_out,
    norm_two,
    mlp_in,
    mlp_out,
    cotangent,
):
    var_index = lax.axis_index("var")
    patch_index = lax.axis_index("patch")
    all_rows, seg_len, var_local, pixels = input_field.shape
    own_rows = cotangent.shape[0]
    model_width = agg_out.shape[0]
    head_dim = model_width // HEADS
    scaling = 1.0 / math.sqrt(head_dim)
    full_len = seg_len * lax.axis_size("patch")
    tokens = own_rows * seg_len
    agg_q = jnp.dot(agg_query[None], query_proj, preferred_element_type=jnp.float32)[0]
    own_counts = lax.dynamic_slice_in_dim(counts, var_index * own_rows, own_rows, 0)
    positions = patch_index * seg_len + jnp.arange(seg_len, dtype=jnp.int32)
    valid_rows = (positions[None, :] < own_counts[:, None]).astype(jnp.float32).reshape(tokens, 1)
    id_part = lax.dynamic_slice_in_dim(var_ids, var_index * var_local, var_local, 1)
    part_max, part_total, part_weighted, kept_front = front_forward(
        input_field, id_part, patch_weight, var_embed, agg_q, key_proj, value_proj
    )
    pieces = (
        lax.all_to_all(
            part_weighted[None].astype(jnp.bfloat16), "var", split_axis=1, concat_axis=0, tiled=True
        ).astype(jnp.float32),
        lax.all_to_all(
            part_max[None].astype(jnp.bfloat16), "var", split_axis=1, concat_axis=0, tiled=True
        ).astype(jnp.float32),
        lax.all_to_all(
            part_total[None].astype(jnp.bfloat16), "var", split_axis=1, concat_axis=0, tiled=True
        ).astype(jnp.float32),
    )
    row_max = jnp.max(pieces[1], axis=0)
    factors = jnp.exp(pieces[1] - row_max[None])
    total_sum = jnp.sum(pieces[2] * factors, axis=0)
    numerator = jnp.sum(pieces[0] * factors[..., None], axis=0)
    mixed_rows = (numerator / total_sum[..., None]).reshape(own_rows, seg_len, model_width)
    log_total = row_max + jnp.log(total_sum)
    mixed_low = mixed_rows.astype(jnp.bfloat16).reshape(tokens, model_width)
    front_out = jnp.dot(mixed_low, agg_out, preferred_element_type=jnp.float32) * valid_rows
    normed_one, norm_one_pull = jax.vjp(layer_norm, front_out, norm_one.astype(jnp.float32))
    normed_one_low = normed_one.astype(jnp.bfloat16)
    triple = jnp.dot(normed_one_low, trunk_qkv, preferred_element_type=jnp.float32).astype(
        jnp.bfloat16
    )
    query_low = triple[:, :model_width].reshape(own_rows, seg_len, HEADS, head_dim)
    key_low = triple[:, model_width : 2 * model_width].reshape(own_rows, seg_len, model_width)
    value_low = triple[:, 2 * model_width :].reshape(own_rows, seg_len, model_width)
    key_all, value_all = (
        lax.all_gather(key_low, "patch", axis=1, tiled=True),
        lax.all_gather(value_low, "patch", axis=1, tiled=True),
    )
    key_heads = key_all.reshape(own_rows, full_len, HEADS, head_dim)
    value_heads = value_all.reshape(own_rows, full_len, HEADS, head_dim)
    key_valid = jnp.arange(full_len, dtype=jnp.int32)[None, :] < own_counts[:, None]
    scores = (
        jnp.einsum("bqhd,bkhd->bhqk", query_low, key_heads, preferred_element_type=jnp.float32)
        * scaling
    )
    masked = jnp.where(key_valid[:, None, None, :], scores, MASKED)
    row_top = jnp.max(masked, axis=-1)
    exponent = jnp.exp(masked - row_top[..., None])
    denominator = jnp.sum(exponent, axis=-1)
    shares_low = (exponent / denominator[..., None]).astype(jnp.bfloat16)
    trunk_log_total = row_top + jnp.log(denominator)
    attended = (
        jnp.einsum("bhqk,bkhd->bqhd", shares_low, value_heads, preferred_element_type=jnp.float32)
        .astype(jnp.bfloat16)
        .reshape(tokens, model_width)
    )
    after_attn = front_out + jnp.dot(attended, trunk_out, preferred_element_type=jnp.float32)
    normed_two, norm_two_pull = jax.vjp(layer_norm, after_attn, norm_two.astype(jnp.float32))
    normed_two_low = normed_two.astype(jnp.bfloat16)
    inner_rows = jnp.dot(normed_two_low, mlp_in, preferred_element_type=jnp.float32)
    active, gelu_pull = jax.vjp(gelu_exact, inner_rows)
    active_low = active.astype(jnp.bfloat16)
    result = after_attn + jnp.dot(active_low, mlp_out, preferred_element_type=jnp.float32)
    block_out = (result * valid_rows).astype(jnp.bfloat16).reshape(own_rows, seg_len, model_width)
    out_grad = cotangent.reshape(tokens, model_width).astype(jnp.float32) * valid_rows
    out_grad_low = out_grad.astype(jnp.bfloat16)
    mlp_out_grad = jnp.einsum(
        "nf,nd->fd", active_low, out_grad_low, preferred_element_type=jnp.float32
    )
    act_grad = jnp.einsum("nd,fd->nf", out_grad_low, mlp_out, preferred_element_type=jnp.float32)
    inner_grad = gelu_pull(act_grad)[0].astype(jnp.bfloat16)
    mlp_in_grad = jnp.einsum(
        "nd,nf->df", normed_two_low, inner_grad, preferred_element_type=jnp.float32
    )
    normed_two_grad = jnp.einsum(
        "nf,df->nd", inner_grad, mlp_in, preferred_element_type=jnp.float32
    )
    after_ln_grad, norm_two_grad = norm_two_pull(normed_two_grad)
    after_grad = out_grad + after_ln_grad
    branch_low = after_grad.astype(jnp.bfloat16)
    trunk_out_grad = jnp.einsum(
        "nd,ne->de", attended, branch_low, preferred_element_type=jnp.float32
    )
    attended_grad = jnp.einsum(
        "ne,de->nd", branch_low, trunk_out, preferred_element_type=jnp.float32
    )
    attended_grad = attended_grad.astype(jnp.bfloat16).reshape(own_rows, seg_len, HEADS, head_dim)
    scores_again = (
        jnp.einsum("bqhd,bkhd->bhqk", query_low, key_heads, preferred_element_type=jnp.float32)
        * scaling
    )
    masked_again = jnp.where(key_valid[:, None, None, :], scores_again, MASKED)
    shares = jnp.exp(masked_again - trunk_log_total[..., None])
    share_grad = jnp.einsum(
        "bqhd,bkhd->bhqk", attended_grad, value_heads, preferred_element_type=jnp.float32
    )
    share_dot = jnp.sum(shares * share_grad, axis=-1, keepdims=True)
    score_grad = (shares * (share_grad - share_dot)).astype(jnp.bfloat16)
    query_grad = (
        jnp.einsum("bhqk,bkhd->bqhd", score_grad, key_heads, preferred_element_type=jnp.float32)
        * scaling
    ).astype(jnp.bfloat16)
    shares_again = shares.astype(jnp.bfloat16)
    value_grad_all = jnp.einsum(
        "bhqk,bqhd->bkhd", shares_again, attended_grad, preferred_element_type=jnp.float32
    )
    key_grad_all = (
        jnp.einsum("bhqk,bqhd->bkhd", score_grad, query_low, preferred_element_type=jnp.float32)
        * scaling
    )
    key_grad, value_grad = (
        lax.psum_scatter(
            key_grad_all.reshape(own_rows, full_len, model_width).astype(jnp.bfloat16),
            "patch",
            scatter_dimension=1,
            tiled=True,
        ).astype(jnp.float32),
        lax.psum_scatter(
            value_grad_all.reshape(own_rows, full_len, model_width).astype(jnp.bfloat16),
            "patch",
            scatter_dimension=1,
            tiled=True,
        ).astype(jnp.float32),
    )
    triple_grad = jnp.concatenate(
        [
            query_grad.reshape(tokens, model_width),
            key_grad.reshape(tokens, model_width).astype(jnp.bfloat16),
            value_grad.reshape(tokens, model_width).astype(jnp.bfloat16),
        ],
        axis=1,
    )
    trunk_qkv_grad = jnp.einsum(
        "nd,ne->de", normed_one_low, triple_grad, preferred_element_type=jnp.float32
    )
    normed_one_grad = jnp.einsum(
        "ne,de->nd", triple_grad, trunk_qkv, preferred_element_type=jnp.float32
    )
    front_ln_grad, norm_one_grad = norm_one_pull(normed_one_grad)
    agg_grad = ((after_grad + front_ln_grad) * valid_rows).astype(jnp.bfloat16)
    agg_out_grad = jnp.einsum("nd,ne->de", mixed_low, agg_grad, preferred_element_type=jnp.float32)
    mixed_grad = jnp.einsum("ne,de->nd", agg_grad, agg_out, preferred_element_type=jnp.float32)
    mixed_grad = mixed_grad.astype(jnp.bfloat16).reshape(own_rows, seg_len, model_width)
    front_delta = jnp.sum(
        (mixed_grad.astype(jnp.float32) * mixed_rows).reshape(own_rows, seg_len, HEADS, head_dim),
        axis=-1,
    )
    mixed_grad_all = lax.all_gather(mixed_grad, "var", axis=0, tiled=True)
    log_total_all, delta_all = (
        lax.all_gather(log_total, "var", axis=0, tiled=True),
        lax.all_gather(front_delta, "var", axis=0, tiled=True),
    )
    field_grad, patch_grad, vembed_grad, aggq_grad, key_proj_grad, value_proj_grad = front_backward(
        input_field,
        kept_front,
        mixed_grad_all,
        log_total_all,
        delta_all,
        agg_q,
        key_proj,
        value_proj,
    )
    query_proj_grad = agg_query.astype(jnp.float32)[:, None] * aggq_grad[None, :]
    agg_query_grad = jnp.dot(query_proj.astype(jnp.float32), aggq_grad, precision=HIGHEST)
    shares_all = (
        lax.psum_scatter(
            patch_grad.astype(jnp.bfloat16), "patch", scatter_dimension=2, tiled=True
        ).astype(jnp.float32),
        lax.psum_scatter(
            vembed_grad.astype(jnp.bfloat16), "patch", scatter_dimension=1, tiled=True
        ).astype(jnp.float32),
        lax.psum_scatter(
            agg_query_grad.astype(jnp.bfloat16), "patch", scatter_dimension=0, tiled=True
        ).astype(jnp.float32),
        lax.psum_scatter(
            query_proj_grad.astype(jnp.bfloat16), "patch", scatter_dimension=0, tiled=True
        ).astype(jnp.float32),
        lax.psum_scatter(
            key_proj_grad.astype(jnp.bfloat16), "patch", scatter_dimension=0, tiled=True
        ).astype(jnp.float32),
        lax.psum_scatter(
            value_proj_grad.astype(jnp.bfloat16), "patch", scatter_dimension=0, tiled=True
        ).astype(jnp.float32),
        lax.psum_scatter(
            agg_out_grad.astype(jnp.bfloat16), "patch", scatter_dimension=0, tiled=True
        ).astype(jnp.float32),
        lax.psum_scatter(
            norm_one_grad.astype(jnp.bfloat16), "patch", scatter_dimension=0, tiled=True
        ).astype(jnp.float32),
        lax.psum_scatter(
            trunk_qkv_grad.astype(jnp.bfloat16), "patch", scatter_dimension=0, tiled=True
        ).astype(jnp.float32),
        lax.psum_scatter(
            trunk_out_grad.astype(jnp.bfloat16), "patch", scatter_dimension=0, tiled=True
        ).astype(jnp.float32),
        lax.psum_scatter(
            norm_two_grad.astype(jnp.bfloat16), "patch", scatter_dimension=0, tiled=True
        ).astype(jnp.float32),
        lax.psum_scatter(
            mlp_in_grad.astype(jnp.bfloat16), "patch", scatter_dimension=0, tiled=True
        ).astype(jnp.float32),
        lax.psum_scatter(
            mlp_out_grad.astype(jnp.bfloat16), "patch", scatter_dimension=0, tiled=True
        ).astype(jnp.float32),
    )
    summed = (
        lax.psum(shares_all[0].astype(jnp.bfloat16), "var").astype(jnp.float32),
        lax.psum(shares_all[1].astype(jnp.bfloat16), "var").astype(jnp.float32),
        lax.psum(shares_all[2].astype(jnp.bfloat16), "var").astype(jnp.float32),
        lax.psum(shares_all[3].astype(jnp.bfloat16), "var").astype(jnp.float32),
        lax.psum(shares_all[4].astype(jnp.bfloat16), "var").astype(jnp.float32),
        lax.psum(shares_all[5].astype(jnp.bfloat16), "var").astype(jnp.float32),
        lax.psum(shares_all[6].astype(jnp.bfloat16), "var").astype(jnp.float32),
        lax.psum(shares_all[7].astype(jnp.bfloat16), "var").astype(jnp.float32),
        lax.psum(shares_all[8].astype(jnp.bfloat16), "var").astype(jnp.float32),
        lax.psum(shares_all[9].astype(jnp.bfloat16), "var").astype(jnp.float32),
        lax.psum(shares_all[10].astype(jnp.bfloat16), "var").astype(jnp.float32),
        lax.psum(shares_all[11].astype(jnp.bfloat16), "var").astype(jnp.float32),
        lax.psum(shares_all[12].astype(jnp.bfloat16), "var").astype(jnp.float32),
    )
    return (
        block_out,
        field_grad,
        summed[0],
        summed[1],
        summed[2],
        summed[3],
        summed[4],
        summed[5],
        summed[6],
        summed[7],
        summed[8],
        summed[9],
        summed[10],
        summed[11],
        summed[12],
    )


def solution(mesh):
    placed = (
        P(None, "patch", "var", None),
        P(),
        P(),
        P(),
        P(),
        P(),
        P(),
        P(),
        P(),
        P(),
        P(),
        P(),
        P(),
        P(),
        P(),
        P(),
        P("var", "patch", None),
    )
    return jax.shard_map(
        local,
        mesh=mesh,
        in_specs=placed,
        out_specs=(
            P("var", "patch", None),
            P(None, "patch", "var", None),
            P(None, None, "patch"),
            P(None, "patch"),
            P("patch"),
            P("patch", None),
            P("patch", None),
            P("patch", None),
            P("patch", None),
            P("patch"),
            P("patch", None),
            P("patch", None),
            P("patch"),
            P("patch", None),
            P("patch", None),
        ),
        check_vma=False,
    )
```

profile of v0, /device:TPU:1, one launch (start us, length us, event | category | flops | bytes accessed | tf_op | source)
XLA Modules:
  0.0 1836.0 jit_solution(6756827012672266294)
XLA Ops:
  14.1 6.5 fusion
  20.6 14.5 copy.113
  35.1 19.8 %reshape.523 = bf16[6144,1024]{1,0:T(8,128)(2,1)} reshape(bf16[4,128,12,1024]{3,2,1,0:T(8,128)(2,1)} %copy.113) | data formatting | bytes 25165824 | tf_op jit(solution)/shard_map/reshape | solution.py:44
  55.0 20.1 %convolution_convert_fusion.1 = bf16[6144,1024]{1,0:T(8,128)(2,1)} fusion(bf16[6144,1024]{1,0:T(8,128)(2,1)} %reshape.523, bf16[1024,1024]{1,0:T(8,128)(2,1)S(1)} %copy-done), kind=kOutput, calls=%fused_computation.14 | convolution fusion | flops 12891193344 | bytes 27262976 | tf_op jit(solution)/shard_map/dot_general | solution.py:45
  75.1 32.7 %reshape.524 = bf16[4,128,12,16,64]{4,3,2,1,0:T(8,128)(2,1)} reshape(bf16[6144,1024]{1,0:T(8,128)(2,1)} %convolution_convert_fusion.1) | data formatting | bytes 25165824 | tf_op jit(solution)/shard_map/reshape | solution.py:52
  107.8 20.5 %multiply_reduce_fusion.3 = f32[4,128,12,16]{3,2,1,0:T(8,128)} fusion(bf16[4,128,12,16,64]{4,3,2,1,0:T(8,128)(2,1)} %reshape.524, f32[16,64]{1,0:T(8,128)S(1)} %mul.353), kind=kLoop, calls=%fused_computation.5 | loop fusion | flops 18776064 | bytes 12980224 | tf_op jit(solution)/shard_map/reduce_sum | solution.py:51
  132.2 4.7 all-to-all-start.1
  136.9 21.3 %convolution_convert_fusion = bf16[6144,1024]{1,0:T(8,128)(2,1)} fusion(bf16[6144,1024]{1,0:T(8,128)(2,1)} %reshape.523, bf16[1024,1024]{1,0:T(8,128)(2,1)} %param.25), kind=kOutput, calls=%fused_computation.13 | convolution fusion | flops 12891193344 | bytes 27262976 | tf_op jit(solution)/shard_map/dot_general | solution.py:46
  161.3 32.7 %reshape.525 = bf16[4,128,12,16,64]{4,3,2,1,0:T(8,128)(2,1)} reshape(bf16[6144,1024]{1,0:T(8,128)(2,1)} %convolution_convert_fusion) | data formatting | bytes 25165824 | tf_op jit(solution)/shard_map/reshape | solution.py:63
  198.0 19.8 %multiply_reduce_fusion.1 = bf16[4,128,16,64]{3,2,1,0:T(8,128)(2,1)} fusion(f32[4,128,16,12]{2,3,1,0:T(8,128)} %get-tuple-element.117, bf16[4,128,12,16,64]{4,3,2,1,0:T(8,128)(2,1)} %reshape.525), kind=kLoop, calls=%fused_computation.1 | loop fusion | flops 18350080 | bytes 14024704
  226.2 12.1 all-to-all-done
  248.4 46.7 %all-gather.11.cloned.1.call-done = bf16[1024,1024]{1,0:T(8,128)(2,1)} async-done(((bf16[128,1024]{1,0:T(8,128)(2,1)}), bf16[1024,1024]{1,0:T(8,128)(2,1)}) %all-gather.11.cloned.1.call-update) | async-done | bytes 2097168 | tf_op jit(solution)/shard_map/all_gather | solution.py:184
  305.4 40.3 %all-gather.9.cloned.1.call-done = bf16[1024,1024]{1,0:T(8,128)(2,1)} async-done(((bf16[128,1024]{1,0:T(8,128)(2,1)}), bf16[1024,1024]{1,0:T(8,128)(2,1)}) %all-gather.9.cloned.1.call-update) | async-done | bytes 2097168 | tf_op jit(solution)/shard_map/all_gather | solution.py:185
  349.6 6.4 fusion.39
  356.9 9.0 multiply_convert_fusion.7
  365.9 7.4 add_convert_fusion.2
  382.2 7.0 fusion.27
  389.2 10.9 copy.158
  404.4 7.2 multiply_reduce_fusion.4
  411.6 4.7 multiply_convert_fusion.4
  419.0 10.9 copy.156
  429.9 4.4 copy.194
  435.7 5.1 fusion.38
  440.8 29.1 %reduce-scatter.39.cloned.1.call-done = bf16[128,1024]{1,0:T(8,128)(2,1)} async-done(((bf16[1024,1024]{1,0:T(8,128)(2,1)}), bf16[128,1024]{1,0:T(8,128)(2,1)}) %reduce-scatter.39.cloned.1.call-update) | async-done | bytes 262160
  472.2 68.6 %reduce-scatter.37.cloned.1.call-done = bf16[128,1024]{1,0:T(8,128)(2,1)} async-done(((bf16[1024,1024]{1,0:T(8,128)(2,1)}), bf16[128,1024]{1,0:T(8,128)(2,1)}) %reduce-scatter.37.cloned.1.call-update) | async-done | bytes 262160
  543.1 6.0 multiply_reduce_fusion.7
  552.4 7.4 all-gather.2
  560.2 5.2 all-gather.4
  565.5 5.1 all-gather.13.cloned.1.call-done
  574.7 18.4 %multiply_reduce_fusion.2 = f32[4,128,12,16]{3,2,1,0:T(8,128)} fusion(bf16[4,128,12,16,64]{4,3,2,1,0:T(8,128)(2,1)} %reshape.525, f32[4,128,16,64]{3,2,1,0:T(8,128)} %reshape.566), kind=kLoop, calls=%fused_computation.4 | loop fusion | flops 18776064 | bytes 15073280 | tf_op jit(solution)/shard_map/reduce_sum | solution.py:82
  593.0 6.7 subtract_multiply_fusion
  599.8 15.5 multiply_convert_fusion.1
  615.3 33.4 %convert_element_type.475 = bf16[6144,1024]{1,0:T(8,128)(2,1)} reshape(bf16[4,128,12,16,64]{4,3,2,1,0:T(8,128)(2,1)} %multiply_convert_fusion.1) | data formatting | bytes 25165824 | tf_op jit(solution)/shard_map/convert_element_type | solution.py:81
  648.7 18.7 %mul.410 = f32[4,128,12,16,64]{4,3,2,1,0:T(8,128)} broadcast(f32[4,128,12,16]{3,2,1,0:T(8,128)} %get-tuple-element.110), dimensions={0,1,2,3} | broadcast | bytes 25559040 | tf_op jit(solution)/shard_map/mul | solution.py:85
  667.4 42.1 %mul.411 = f32[6144,1024]{1,0:T(8,128)} reshape(f32[4,128,12,16,64]{4,3,2,1,0:T(8,128)} %mul.410) | data formatting | bytes 50331648 | tf_op jit(solution)/shard_map/mul | solution.py:85
  709.5 22.8 %fusion.1 = f32[6144,1024]{1,0:T(8,128)} fusion(bf16[1024,1024]{1,0:T(8,128)(2,1)S(1)} %copy-done, f32[6144,1024]{1,0:T(8,128)} %mul.411, f32[1024]{0:T(1024)S(1)} %broadcast_multiply_fusion.2), kind=kOutput, calls=%fused_computation.11 | convolution fusion | flops 12897484800 | bytes 52432896 | tf_op jit(solution)/shard_map/ne,de->nd/dot_general | solution.py:103
  732.2 24.0 %add_convert_fusion = bf16[6144,1024]{1,0:T(8,128)(2,1)} fusion(f32[6144,1024]{1,0:T(8,128)} %fusion.1, bf16[6144,1024]{1,0:T(8,128)(2,1)} %convert_element_type.475, bf16[1024,1024]{1,0:T(8,128)(2,1)} %param.25), kind=kOutput, calls=%fused_computation.7 | convolution fusion | flops 12897484800 | bytes 52428800 | tf_op jit(solution)/shard_map/ne,de->nd/dot_general | solution.py:105
  756.2 19.7 %reshape.537 = bf16[4,128,12,1024]{3,2,1,0:T(8,128)(2,1)} reshape(bf16[6144,1024]{1,0:T(8,128)(2,1)} %add_convert_fusion) | data formatting | bytes 25165824 | tf_op jit(solution)/shard_map/reshape | solution.py:106
  775.9 22.0 %fusion.30 = f32[4,12,16,1024]{3,2,1,0:T(8,128)S(1)} fusion(bf16[4,128,12,16]{1,3,2,0:T(8,128)(2,1)S(1)} %copy-done.35, bf16[4,128,12,1024]{3,2,1,0:T(8,128)(2,1)} %reshape.537), kind=kOutput, calls=%fused_computation.71 | convolution fusion | flops 201326592 | bytes 15925248 | tf_op jit(solution)/shard_map/bljx,bljd->bjxd/dot_general | solution.py:110
  797.9 5.1 bitcast_convert_fusion
  803.0 6.0 copy.160
  809.1 7.1 reshape.572
  820.5 17.2 multiply_reduce_fusion
  839.6 19.1 %convolution_convert_fusion.6 = bf16[1024,1024]{1,0:T(8,128)(2,1)} fusion(bf16[6144,1024]{1,0:T(8,128)(2,1)} %reshape.523, bf16[6144,1024]{1,0:T(8,128)(2,1)} %convert_element_type.475), kind=kOutput, calls=%fused_computation.68 | convolution fusion | flops 12885950464 | bytes 27262976 | tf_op jit(solution)/shard_map/nd,ne->de/dot_general | solution.py:100
  858.7 18.1 multiply_convert_fusion
  876.8 33.5 %convert_element_type.490 = bf16[6144,1024]{1,0:T(8,128)(2,1)} reshape(bf16[4,128,12,16,64]{4,3,2,1,0:T(8,128)(2,1)} %multiply_convert_fusion) | data formatting | bytes 25165824 | tf_op jit(solution)/shard_map/convert_element_type | solution.py:86
  910.3 18.9 %convolution_convert_fusion.7 = bf16[1024,1024]{1,0:T(8,128)(2,1)} fusion(bf16[6144,1024]{1,0:T(8,128)(2,1)} %reshape.523, bf16[6144,1024]{1,0:T(8,128)(2,1)} %convert_element_type.490), kind=kOutput, calls=%fused_computation.69 | convolution fusion | flops 12885950464 | bytes 27262976 | tf_op jit(solution)/shard_map/nd,ne->de/dot_general | solution.py:99
  930.5 4.6 convolution_convert_fusion.4
  936.1 7.0 convolution_convert_fusion.3
  944.0 6.9 convolution_convert_fusion.2
  951.0 7.2 convert_reduce_fusion
  962.1 57.9 %reduce-scatter.27.cloned.1.call-done = bf16[128,1024]{1,0:T(8,128)(2,1)} async-done(((bf16[1024,1024]{1,0:T(8,128)(2,1)}), bf16[128,1024]{1,0:T(8,128)(2,1)}) %reduce-scatter.27.cloned.1.call-update) | async-done | bytes 262160 | tf_op jit(solution)/shard_map/reduce_scatter | solution.py:332
  1020.1 71.2 %reduce-scatter.21.cloned.1.call-done = bf16[128,1024]{1,0:T(8,128)(2,1)} async-done(((bf16[1024,1024]{1,0:T(8,128)(2,1)}), bf16[128,1024]{1,0:T(8,128)(2,1)}) %reduce-scatter.21.cloned.1.call-update) | async-done | bytes 262160 | tf_op jit(solution)/shard_map/reduce_scatter | solution.py:323
  1091.3 70.7 %reduce-scatter.25.cloned.1.call-done = bf16[128,1024]{1,0:T(8,128)(2,1)} async-done(((bf16[1024,1024]{1,0:T(8,128)(2,1)}), bf16[128,1024]{1,0:T(8,128)(2,1)}) %reduce-scatter.25.cloned.1.call-update) | async-done | bytes 262160 | tf_op jit(solution)/shard_map/reduce_scatter | solution.py:329
  1161.9 71.4 %reduce-scatter.23.cloned.1.call-done = bf16[128,1024]{1,0:T(8,128)(2,1)} async-done(((bf16[1024,1024]{1,0:T(8,128)(2,1)}), bf16[128,1024]{1,0:T(8,128)(2,1)}) %reduce-scatter.23.cloned.1.call-update) | async-done | bytes 262160 | tf_op jit(solution)/shard_map/reduce_scatter | solution.py:326
  1233.3 121.9 %reduce-scatter.29.cloned.1.call-done = bf16[128,3072]{1,0:T(8,128)(2,1)} async-done(((bf16[1024,3072]{1,0:T(8,128)(2,1)}), bf16[128,3072]{1,0:T(8,128)(2,1)}) %reduce-scatter.29.cloned.1.call-update) | async-done | bytes 786448 | tf_op jit(solution)/shard_map/reduce_scatter | solution.py:338
  1355.2 153.1 %reduce-scatter.33.cloned.1.call-done = bf16[128,4096]{1,0:T(8,128)(2,1)} async-done(((bf16[1024,4096]{1,0:T(8,128)(2,1)}), bf16[128,4096]{1,0:T(8,128)(2,1)}) %reduce-scatter.33.cloned.1.call-update) | async-done | bytes 1048592 | tf_op jit(solution)/shard_map/reduce_scatter | solution.py:347
  1508.3 151.5 %reduce-scatter.35.cloned.1.call-done = bf16[512,1024]{1,0:T(8,128)(2,1)} async-done(((bf16[4096,1024]{1,0:T(8,128)(2,1)}), bf16[512,1024]{1,0:T(8,128)(2,1)}) %reduce-scatter.35.cloned.1.call-update) | async-done | bytes 1048592 | tf_op jit(solution)/shard_map/reduce_scatter | solution.py:350
  1661.7 5.7 fusion.43
  1670.9 16.5 all-reduce.3
  1687.6 14.6 fusion.44
  1702.1 20.1 %reduce-scatter.43.cloned.1.call-done = bf16[128,48]{1,0:T(8,128)(2,1)} async-done(((bf16[1024,48]{1,0:T(8,128)(2,1)}), bf16[128,48]{1,0:T(8,128)(2,1)}) %reduce-scatter.43.cloned.1.call-update) | async-done | bytes 12304
  1723.0 11.7 all-reduce.4
  1736.9 79.9 %all-reduce.8.cloned.1.call-done = (bf16[48,16,128]{2,0,1:T(8,128)(2,1)}, bf16[128,1024]{1,0:T(8,128)(2,1)}, bf16[128,1024]{1,0:T(8,128)(2,1)}, bf16[128,1024]{1...) async-done(((bf16[48,16,128]{2,0,1:T(8,128)(2,1)}, ...) | async-done | bytes 4390928 | tf_op jit(solution)/shard_map/psum | solution.py:355
  (283 shorter events, 114.2 us)
Async XLA Ops:
  7.2 47.8 %copy-start = (bf16[1024,1024]{1,0:T(8,128)(2,1)S(1)}, bf16[1024,1024]{1,0:T(8,128)(2,1)}, u32[]{:S(2)}) copy-start(bf16[1024,1024]{1,0:T(8,128)(2,1)} %param.24) | copy-start | bytes 6291460
  7.2 2.9 copy-start.66
  7.2 3.0 copy-start.44
  10.0 10.6 copy-start.49
  10.0 4.0 copy-start.34
  10.1 97.7 %copy-start.45 = (f32[16,64]{1,0:T(8,128)}, f32[16,64]{1,0:T(8,128)S(1)}, u32[]{:S(2)}) copy-start(f32[16,64]{1,0:T(8,128)S(1)} %mul.353) | copy-start | bytes 12292
  10.2 10.5 copy-start.47
  14.1 6.6 copy-start.14
  132.2 62.4 %all-to-all-start.1 = ((bf16[1,4,128,16]{2,3,0,1:T(8,128)(2,1)}), bf16[1,4,128,16]{2,3,0,1:T(8,128)(2,1)S(1)}, u32[]{:S(2)}, u32[]{:S(2)}) async-start(bf16[1,4,128,16]{2,3,0,1:T(8,128)(2,1)} %copy.114), calls=%async_computation.1 | async-start | bytes 32768 | tf_op jit(solution)/shard_map/all_to_all | solution.py:160
  136.9 21.3 %copy-start.2 = (f32[4,128,12,16]{3,2,1,0:T(8,128)S(1)}, f32[4,128,12,16]{3,2,1,0:T(8,128)}, u32[]{:S(2)}) copy-start(f32[4,128,12,16]{3,2,1,0:T(8,128)} %multiply_reduce_fusion.3) | copy-start | bytes 1179652
  194.6 26.7 %all-to-all-start.2 = ((bf16[1,4,128,16]{2,3,0,1:T(8,128)(2,1)}), bf16[1,4,128,16]{2,3,0,1:T(8,128)(2,1)S(1)}, u32[]{:S(2)}, u32[]{:S(2)}) async-start(bf16[1,4,128,16]{2,3,0,1:T(8,128)(2,1)} %copy.117), calls=%async_computation.2 | async-start | bytes 32768 | tf_op jit(solution)/shard_map/all_to_all | solution.py:163
  217.7 7.1 copy-start.63
  217.7 7.2 copy-start.67
  221.3 17.1 all-to-all-start
  224.8 70.3 %all-gather.11.cloned.1.call-start = ((), (), s32[]{:S(2)}) async-start(), calls=%async_computation.24 | async-start | bytes 2359296 | tf_op jit(solution)/shard_map/all_gather | solution.py:184
  224.9 324.2 %copy-start.40 = (f32[1024]{0:T(1024)}, f32[1024]{0:T(1024)S(1)}, u32[]{:S(2)}) copy-start(f32[1024]{0:T(1024)S(1)} %convert_element_type.435) | copy-start | bytes 12292
  226.2 323.2 %copy-start.51 = (f32[128]{0:T(128)}, f32[128]{0:T(128)S(1)}, u32[]{:S(2)}) copy-start(f32[128]{0:T(128)S(1)} %compare_convert_fusion) | copy-start | bytes 1540
  238.7 196.0 %copy-start.12 = (f32[128,16,64]{0,2,1:T(8,128)}, f32[128,16,64]{0,2,1:T(8,128)S(1)}, u32[]{:S(2)}) copy-start(f32[128,16,64]{0,2,1:T(8,128)S(1)} %broadcast_divide_fusion) | copy-start | bytes 1572868
  240.7 308.4 %copy-start.5 = (f32[128,1024]{1,0:T(8,128)}, f32[128,1024]{1,0:T(8,128)S(1)}, u32[]{:S(2)}) copy-start(f32[128,1024]{1,0:T(8,128)S(1)} %get-tuple-element.122) | copy-start | bytes 1572868
  240.7 308.4 %copy-start.53 = (f32[128]{0:T(128)}, f32[128]{0:T(128)S(1)}, u32[]{:S(2)}) copy-start(f32[128]{0:T(128)S(1)} %broadcast_multiply_fusion.4) | copy-start | bytes 1540
  240.9 308.1 %copy-start.57 = (f32[128]{0:T(128)}, f32[128]{0:T(128)S(1)}, u32[]{:S(2)}) copy-start(f32[128]{0:T(128)S(1)} %fusion.75) | copy-start | bytes 1540
  245.7 99.9 %all-gather.9.cloned.1.call-start = ((), (), s32[]{:S(2)}) async-start(), calls=%async_computation.23 | async-start | bytes 2359296 | tf_op jit(solution)/shard_map/all_gather | solution.py:185
  246.5 223.4 %reduce-scatter.39.cloned.1.call-start = ((), (), s32[]{:S(2)}) async-start(), calls=%async_computation.27 | async-start | bytes 2359296
  246.6 130.3 %copy-start.42 = (f32[1024]{0:T(1024)}, f32[1024]{0:T(1024)S(1)}, u32[]{:S(2)}) copy-start(f32[1024]{0:T(1024)S(1)} %convert_element_type.442) | copy-start | bytes 12292
  248.4 50.8 %copy-start.24 = (bf16[128,1024]{0,1:T(8,128)(2,1)}, bf16[128,1024]{0,1:T(8,128)(2,1)S(1)}, u32[]{:S(2)}) copy-start(bf16[128,1024]{0,1:T(8,128)(2,1)S(1)} %copy.122) | copy-start | bytes 786436
  302.2 3.2 copy-start.1
  349.6 6.4 copy-start.9
  349.6 16.3 slice-start
  349.6 23.7 %slice-start.2 = ((s8[8388608]{0:T(1024)(128)(4,1)}), s8[4194304]{0:T(1024)(128)(4,1)S(1)}, s32[]{:S(2)}) async-start(s8[8388608]{0:T(1024)(128)(4,1)} %bitcast.195), calls=%async_computation.33 | async-start | bytes 8388608
  356.6 20.3 %copy-start.7 = (f32[128,1024]{1,0:T(8,128)}, f32[128,1024]{1,0:T(8,128)S(1)}, u32[]{:S(2)}) copy-start(f32[128,1024]{1,0:T(8,128)S(1)} %get-tuple-element.126) | copy-start | bytes 1572868
  356.6 20.3 %copy-start.55 = (f32[128]{0:T(128)}, f32[128]{0:T(128)S(1)}, u32[]{:S(2)}) copy-start(f32[128]{0:T(128)S(1)} %broadcast_multiply_fusion.3) | copy-start | bytes 1540
  356.9 20.1 %copy-start.59 = (f32[128]{0:T(128)}, f32[128]{0:T(128)S(1)}, u32[]{:S(2)}) copy-start(f32[128]{0:T(128)S(1)} %fusion.76) | copy-start | bytes 1540
  356.9 9.0 slice-start.1
  356.9 9.0 copy-start.18
  356.9 16.5 slice-start.3
  373.4 3.5 copy-start.17
  404.4 136.4 %reduce-scatter.37.cloned.1.call-start = ((), (), s32[]{:S(2)}) async-start(), calls=%async_computation.26 | async-start | bytes 2359296
  411.6 4.7 copy-start.25
  416.3 2.6 copy-start.3
  434.3 136.3 %all-gather.13.cloned.1.call-start = ((), (), s32[]{:S(2)}) async-start(), calls=%async_computation.25 | async-start | bytes 1310720 | tf_op jit(solution)/shard_map/all_gather | solution.py:296
  543.1 6.3 copy-start.16
  552.3 407.2 %reduce-scatter.41.cloned.1.call-start = ((), (), s32[]{:S(2)}) async-start(), calls=%async_computation.28 | async-start | bytes 1769472
  593.0 6.7 copy-start.4
  756.2 19.7 %copy-start.35 = (bf16[4,128,12,16]{1,3,2,0:T(8,128)(2,1)S(1)}, bf16[4,128,12,16]{1,3,2,0:T(8,128)(2,1)}, u32[]{:S(2)}) copy-start(bf16[4,128,12,16]{1,3,2,0:T(8,128)(2,1)} %param.17) | copy-start | bytes 589828
  775.9 22.0 %copy-start.48 = (s32[4,12]{1,0:T(4,128)S(1)}, s32[4,12]{1,0:T(4,128)}, u32[]{:S(2)}) copy-start(s32[4,12]{1,0:T(4,128)} %copy-done.47) | copy-start | bytes 580
  809.1 7.2 copy-start.21
  809.1 7.2 copy-start.31
  816.2 145.9 %reduce-scatter.31.cloned.1.call-start = ((), (), s32[]{:S(2)}) async-start(), calls=%async_computation.20 | async-start | bytes 2359296 | tf_op jit(solution)/shard_map/reduce_scatter | solution.py:341
  818.3 201.8 %reduce-scatter.27.cloned.1.call-start = ((), (), s32[]{:S(2)}) async-start(), calls=%async_computation.18 | async-start | bytes 2359296 | tf_op jit(solution)/shard_map/reduce_scatter | solution.py:332
  820.5 270.8 %reduce-scatter.21.cloned.1.call-start = ((), (), s32[]{:S(2)}) async-start(), calls=%async_computation.15 | async-start | bytes 2359296 | tf_op jit(solution)/shard_map/reduce_scatter | solution.py:323
  839.5 322.4 %reduce-scatter.25.cloned.1.call-start = ((), (), s32[]{:S(2)}) async-start(), calls=%async_computation.17 | async-start | bytes 2359296 | tf_op jit(solution)/shard_map/reduce_scatter | solution.py:329
  858.7 374.7 %reduce-scatter.23.cloned.1.call-start = ((), (), s32[]{:S(2)}) async-start(), calls=%async_computation.16 | async-start | bytes 2359296 | tf_op jit(solution)/shard_map/reduce_scatter | solution.py:326
  929.3 425.9 %reduce-scatter.29.cloned.1.call-start = ((), (), s32[]{:S(2)}) async-start(), calls=%async_computation.19 | async-start | bytes 7077888 | tf_op jit(solution)/shard_map/reduce_scatter | solution.py:338
  935.1 573.2 %reduce-scatter.33.cloned.1.call-start = ((), (), s32[]{:S(2)}) async-start(), calls=%async_computation.21 | async-start | bytes 9437184 | tf_op jit(solution)/shard_map/reduce_scatter | solution.py:347
  943.1 716.7 %reduce-scatter.35.cloned.1.call-start = ((), (), s32[]{:S(2)}) async-start(), calls=%async_computation.22 | async-start | bytes 9437184 | tf_op jit(solution)/shard_map/reduce_scatter | solution.py:350
  950.9 771.3 %reduce-scatter.43.cloned.1.call-start = ((), (), s32[]{:S(2)}) async-start(), calls=%async_computation.29 | async-start | bytes 294912
  959.4 857.4 %all-reduce.8.cloned.1.call-start = ((), (), s32[]{:S(2)}) async-start(), calls=%async_computation.30 | async-start | bytes 8781824 | tf_op jit(solution)/shard_map/psum | solution.py:355
  1667.4 3.4 copy-start.62
  1667.4 3.4 copy-start.65
  1816.8 5.5 copy-start.39
  1816.8 6.3 copy-start.38
  1816.8 7.1 copy-start.37
  1818.6 6.2 copy-start.36
  1823.1 3.0 copy-start.28
  (28 other events, 37.1 us)
Sparse Core Ops, SparseCore 0:
  245.9 49.1 all-gather.10
  297.8 47.8 all-gather.8
  404.5 65.3 reduce-scatter.38
  473.9 66.8 reduce-scatter.36
  552.4 18.1 all-gather.12
  816.3 63.0 reduce-scatter.40
  883.4 66.0 reduce-scatter.30
  953.4 66.5 reduce-scatter.26
  1024.6 66.5 reduce-scatter.20
  1095.0 66.8 reduce-scatter.24
  1166.4 66.8 reduce-scatter.22
  1237.2 117.9 reduce-scatter.28
  1359.3 148.9 reduce-scatter.32
  1511.8 148.0 reduce-scatter.34
  1664.0 58.2 reduce-scatter.42
  1726.0 90.7 all-reduce.7
where the time goes:
time: 1850 us; the launch traced here: 1840 us
  waiting for transfers between devices  1000 us (54%)
  local copies, waits for them, and re-layouts  335 us (18%)
  matrix products  277 us (15%)
  other arithmetic  154 us (8%)
  blocking collectives  40.8 us (2%)
    reduce_scatter x1, waiting for transfers between devices, local(): lax.psum_scatter(mlp_in_grad.astype(jnp.bfloat16), 'patch', scatter_dimen...  153 us
    reduce_scatter x1, waiting for transfers between devices, local(): lax.psum_scatter(mlp_out_grad.astype(jnp.bfloat16), 'patch', scatter_dime...  152 us
    reduce_scatter x1, waiting for transfers between devices, local(): lax.psum_scatter(trunk_qkv_grad.astype(jnp.bfloat16), 'patch', scatter_di...  122 us
    unnamed x20, waiting for transfers between devices  119 us
    psum x1, waiting for transfers between devices, local(): lax.psum(shares_all[0].astype(jnp.bfloat16), 'var').astype(jnp.float32)  79.9 us
    reduce_scatter x1, waiting for transfers between devices, local(): lax.psum_scatter(key_proj_grad.astype(jnp.bfloat16), 'patch', scatter_dim...  71.4 us
    reduce_scatter x1, waiting for transfers between devices, local(): lax.psum_scatter(query_proj_grad.astype(jnp.bfloat16), 'patch', scatter_d...  71.2 us
    reduce_scatter x1, waiting for transfers between devices, local(): lax.psum_scatter(value_proj_grad.astype(jnp.bfloat16), 'patch', scatter_d...  70.7 us
  transfers between devices with their start and end apart: 19, of which 15 were waited for; matrix products, arithmetic and copies ran while one was open for 16% of the time, Pallas kernels for 0%

commit v1 on v0

v1 whole, which is shorter than its diff:
```python
import functools
import math

import jax
import jax.numpy as jnp
from jax import lax
from jax.experimental import pallas as pl
from jax.experimental.pallas import tpu as pltpu
from jax.sharding import PartitionSpec as P

HEADS = 16
VARS = 48
EPSILON = 1e-05
MASKED = -1e30
HIGHEST = lax.Precision.HIGHEST
BF16 = jnp.bfloat16
F32 = jnp.float32
NN = (((1,), (0,)), ((), ()))
NT = (((1,), (1,)), ((), ()))
TN = (((0,), (0,)), ((), ()))


def mm(a, b, dims=NN, precision=None):
    return lax.dot_general(a, b, dims, precision=precision, preferred_element_type=F32)


def layer_norm(values, gain_vec):
    average = jnp.mean(values, axis=-1, keepdims=True)
    center = values - average
    spread = jnp.mean(center * center, axis=-1, keepdims=True)
    return center * lax.rsqrt(spread + EPSILON) * gain_vec


def gelu_exact(values):
    return jax.nn.gelu(values, approximate=False)


def split_high_low(values):
    high = values.astype(BF16)
    return high, (values - high.astype(F32)).astype(BF16)


def front_forward_kernel(
    pixels, ids_ref, field_ref, spread_ref, bias_ref, vwt_ref, vet_ref, x_ref, p_ref, mixed_ref, mt_ref
):
    seg = field_ref.shape[1]
    head_dim = mixed_ref.shape[1] // HEADS
    for slot in range(VARS):
        start = pl.multiple_of(ids_ref[0, slot] * pixels, pixels)
        x_ref[pl.ds(start, pixels), :] = field_ref[slot * pixels : (slot + 1) * pixels, :]
    scores = mm(spread_ref[...], x_ref[...]) + bias_ref[...]
    scores = scores.reshape(HEADS, VARS, seg)
    top = jnp.max(scores, axis=1, keepdims=True)
    exponent = jnp.exp(scores - top)
    total = jnp.sum(exponent, axis=1, keepdims=True)
    p_ref[...] = (exponent * (1.0 / total)).reshape(HEADS * VARS, seg)

    def head(h, carry):
        shares = p_ref[pl.ds(pl.multiple_of(h * VARS, VARS), VARS), :]
        pix = x_ref[...].astype(F32).reshape(VARS, pixels, seg)
        scaled = (pix * shares[:, None, :]).astype(BF16).reshape(VARS * pixels, seg)
        rows = pl.ds(pl.multiple_of(h * head_dim, head_dim), head_dim)
        mt_ref[rows, :] = mm(vwt_ref[rows, :], scaled) + mm(vet_ref[rows, :], shares.astype(BF16))
        return carry

    lax.fori_loop(0, HEADS, head, 0)
    mixed_ref[...] = mt_ref[...].T.astype(BF16)


def front_forward(own_ids, own_field, spread, bias, vwt, vet):
    rows, seg = own_field.shape
    width = vwt.shape[0]
    vmem = pl.BlockSpec(memory_space=pltpu.VMEM)
    return pl.pallas_call(
        functools.partial(front_forward_kernel, rows // VARS),
        out_shape=(
            jax.ShapeDtypeStruct((rows, seg), BF16),
            jax.ShapeDtypeStruct((HEADS * VARS, seg), F32),
            jax.ShapeDtypeStruct((seg, width), BF16),
        ),
        in_specs=[pl.BlockSpec(memory_space=pltpu.SMEM)] + [vmem] * 5,
        out_specs=(vmem,) * 3,
        scratch_shapes=[pltpu.VMEM((width, seg), F32)],
        name="front_forward",
    )(own_ids, own_field, spread, bias, vwt, vet)


def front_backward_kernel(
    pixels,
    ids_ref,
    x_ref,
    p_ref,
    mg_ref,
    vw_ref,
    ve_ref,
    spread_ref,
    field_ref,
    m_ref,
    me_ref,
    s_ref,
    se_ref,
    fs_ref,
    dx_ref,
):
    rows, seg = x_ref.shape
    width = mg_ref.shape[1]
    head_dim = width // HEADS
    pair_dim = 2 * head_dim
    lane = lax.broadcasted_iota(jnp.int32, (seg, pair_dim), 1)
    dx_ref[...] = jnp.zeros_like(dx_ref)

    def pair(q, carry):
        cols = pl.ds(pl.multiple_of(q * pair_dim, pair_dim), pair_dim)
        grad = mg_ref[:, cols]
        none = jnp.zeros_like(grad)
        both = jnp.concatenate(
            [jnp.where(lane < head_dim, grad, none), jnp.where(lane >= head_dim, grad, none)], axis=0
        )
        inner = mm(vw_ref[:, cols], both, NT)
        inner_e = mm(ve_ref[:, cols], both, NT)
        pix = x_ref[...].astype(F32).reshape(VARS, pixels, seg)
        scaled, weights = [], []
        for k in range(2):
            hrows = pl.ds(pl.multiple_of((2 * q + k) * VARS, VARS), VARS)
            shares = p_ref[hrows, :]
            part = inner[:, k * seg : (k + 1) * seg].reshape(VARS, pixels, seg)
            share_grad = jnp.sum(pix * part, axis=1) + inner_e[:, k * seg : (k + 1) * seg]
            delta = jnp.sum(shares * share_grad, axis=0, keepdims=True)
            fs_ref[hrows, :] = shares * (share_grad - delta)
            wide = shares[:, None, :]
            dx_ref[...] += (part * wide).reshape(rows, seg)
            scaled.append((pix * wide).astype(BF16).reshape(rows, seg))
            weights.append(shares.astype(BF16))
        m_ref[:, cols] = mm(jnp.concatenate(scaled, axis=1), both).astype(BF16)
        me_ref[:, cols] = mm(jnp.concatenate(weights, axis=1), both).astype(BF16)
        return carry

    lax.fori_loop(0, HEADS // 2, pair, 0)
    score_grad = fs_ref[...]
    low = score_grad.astype(BF16)
    dx = dx_ref[...] + mm(spread_ref[...], low, TN)
    dx_ref[...] = dx
    for slot in range(VARS):
        start = pl.multiple_of(ids_ref[0, slot] * pixels, pixels)
        field_ref[slot * pixels : (slot + 1) * pixels, :] = dx_ref[pl.ds(start, pixels), :].astype(BF16)
    se_ref[...] = jnp.sum(score_grad, axis=1, keepdims=True)
    var_row = lax.broadcasted_iota(jnp.int32, (VARS, rows), 0)
    var_col = lax.broadcasted_iota(jnp.int32, (VARS, rows), 1) // pixels
    keep = var_row == var_col
    for h in range(HEADS):
        outer = mm(low[h * VARS : (h + 1) * VARS, :], x_ref[...], NT)
        s_ref[h : h + 1, :] = jnp.sum(jnp.where(keep, outer, 0.0), axis=0, keepdims=True)


def front_backward(own_ids, x_own, shares, mixed_grad, vw, ve, spread):
    rows, seg = x_own.shape
    width = mixed_grad.shape[1]
    vmem = pl.BlockSpec(memory_space=pltpu.VMEM)
    return pl.pallas_call(
        functools.partial(front_backward_kernel, rows // VARS),
        out_shape=(
            jax.ShapeDtypeStruct((rows, seg), BF16),
            jax.ShapeDtypeStruct((rows, width), BF16),
            jax.ShapeDtypeStruct((VARS, width), BF16),
            jax.ShapeDtypeStruct((HEADS, rows), F32),
            jax.ShapeDtypeStruct((HEADS * VARS, 1), F32),
        ),
        in_specs=[pl.BlockSpec(memory_space=pltpu.SMEM)] + [vmem] * 6,
        out_specs=(vmem,) * 5,
        scratch_shapes=[pltpu.VMEM((HEADS * VARS, seg), F32), pltpu.VMEM((rows, seg), F32)],
        name="front_backward",
    )(own_ids, x_own, shares, mixed_grad, vw, ve, spread)


def load_parts(ref, part, seg, out_ref):
    for source in range(ref.shape[0]):
        out_ref[source * seg : (source + 1) * seg, :] = ref[source, part * seg : (part + 1) * seg, :]


def attend_forward_kernel(head_dim, block, count_ref, qkv_ref, out_ref, lse_ref, q_ref, k_ref, vt_ref):
    full, width = q_ref.shape
    seg = full // qkv_ref.shape[0]
    scaling = 1.0 / math.sqrt(head_dim)
    load_parts(qkv_ref, 2, seg, q_ref)
    vt_ref[...] = q_ref[...].T
    load_parts(qkv_ref, 0, seg, q_ref)
    load_parts(qkv_ref, 1, seg, k_ref)
    count = count_ref[0, 0]
    lane = lax.broadcasted_iota(jnp.int32, (block, width), 1) // head_dim
    row = lax.broadcasted_iota(jnp.int32, (width, block), 0) // head_dim
    valid = lax.broadcasted_iota(jnp.int32, (full, block), 0) < count

    def step(i, carry):
        part = pl.ds(pl.multiple_of(i * block, block), block)
        query = q_ref[part, :]
        total = jnp.zeros((width, block), F32)
        for h in range(width // head_dim):
            own = jnp.where(lane == h, query, jnp.zeros_like(query))
            scores = jnp.where(valid, mm(k_ref[...], own, NT) * scaling, MASKED)
            top = jnp.max(scores, axis=0, keepdims=True)
            exponent = jnp.exp(scores - top)
            denominator = jnp.sum(exponent, axis=0, keepdims=True)
            shares = (exponent * (1.0 / denominator)).astype(BF16)
            lse_ref[h : h + 1, part] = top + jnp.log(denominator)
            total = jnp.where(row == h, mm(vt_ref[...], shares), total)
        out_ref[part, :] = total.T.astype(BF16)
        return carry

    lax.fori_loop(0, full // block, step, 0)


def attend_forward(count, qkv, head_dim):
    parts, triple_rows, width = qkv.shape
    full = parts * triple_rows // 3
    vmem = pl.BlockSpec(memory_space=pltpu.VMEM)
    block = min(256, full)
    return pl.pallas_call(
        functools.partial(attend_forward_kernel, head_dim, block),
        out_shape=(
            jax.ShapeDtypeStruct((full, width), BF16),
            jax.ShapeDtypeStruct((width // head_dim, full), F32),
        ),
        in_specs=[pl.BlockSpec(memory_space=pltpu.SMEM), vmem],
        out_specs=(vmem, vmem),
        scratch_shapes=[
            pltpu.VMEM((full, width), BF16),
            pltpu.VMEM((full, width), BF16),
            pltpu.VMEM((width, full), BF16),
        ],
        name="attend_forward",
    )(count, qkv)


def attend_backward_kernel(
    head_dim, block, count_ref, qkv_ref, grad_ref, lse_ref, out_ref, q_ref, k_ref, v_ref, kt_ref, dk_ref, dv_ref
):
    full, width = q_ref.shape
    seg = full // qkv_ref.shape[0]
    scaling = 1.0 / math.sqrt(head_dim)
    load_parts(qkv_ref, 0, seg, q_ref)
    load_parts(qkv_ref, 1, seg, k_ref)
    load_parts(qkv_ref, 2, seg, v_ref)
    kt_ref[...] = k_ref[...].T
    dk_ref[...] = jnp.zeros_like(dk_ref)
    dv_ref[...] = jnp.zeros_like(dv_ref)
    count = count_ref[0, 0]
    lane = lax.broadcasted_iota(jnp.int32, (block, width), 1) // head_dim
    row = lax.broadcasted_iota(jnp.int32, (width, block), 0) // head_dim
    valid = lax.broadcasted_iota(jnp.int32, (full, block), 0) < count

    def step(i, carry):
        part = pl.ds(pl.multiple_of(i * block, block), block)
        query = q_ref[part, :]
        grad = grad_ref[part, :]
        total = jnp.zeros((width, block), F32)
        for h in range(width // head_dim):
            own = jnp.where(lane == h, query, jnp.zeros_like(query))
            own_grad = jnp.where(lane == h, grad, jnp.zeros_like(grad))
            scores = jnp.where(valid, mm(k_ref[...], own, NT) * scaling, MASKED)
            shares = jnp.exp(scores - lse_ref[h : h + 1, part])
            share_grad = mm(v_ref[...], own_grad, NT)
            dot = jnp.sum(shares * share_grad, axis=0, keepdims=True)
            score_grad = (shares * (share_grad - dot)).astype(BF16)
            dv_ref[...] += mm(shares.astype(BF16), own_grad)
            dk_ref[...] += mm(score_grad, own)
            total = jnp.where(row == h, mm(kt_ref[...], score_grad), total)
        turned = (total * scaling).T.astype(BF16)
        for piece in range(block // seg):
            out_ref[i * (block // seg) + piece, 0:seg, :] = turned[piece * seg : (piece + 1) * seg, :]
        return carry

    lax.fori_loop(0, full // block, step, 0)
    for source in range(full // seg):
        rows = slice(source * seg, (source + 1) * seg)
        out_ref[source, seg : 2 * seg, :] = (dk_ref[rows, :] * scaling).astype(BF16)
        out_ref[source, 2 * seg : 3 * seg, :] = dv_ref[rows, :].astype(BF16)


def attend_backward(count, qkv, grad, lse, head_dim):
    parts, triple_rows, width = qkv.shape
    full = parts * triple_rows // 3
    vmem = pl.BlockSpec(memory_space=pltpu.VMEM)
    block = min(256, full)
    return pl.pallas_call(
        functools.partial(attend_backward_kernel, head_dim, block),
        out_shape=jax.ShapeDtypeStruct(qkv.shape, BF16),
        in_specs=[pl.BlockSpec(memory_space=pltpu.SMEM), vmem, vmem, vmem],
        out_specs=vmem,
        scratch_shapes=[pltpu.VMEM((full, width), BF16)] * 3
        + [pltpu.VMEM((width, full), BF16)]
        + [pltpu.VMEM((full, width), F32)] * 2,
        name="attend_backward",
    )(count, qkv, grad, lse)


def gathered_attention(triple, count, head_dim):
    seg, triple_width = triple.shape
    width = triple_width // 3
    scaling = 1.0 / math.sqrt(head_dim)
    full = seg * lax.axis_size("patch")
    query = triple[:, :width].reshape(seg, HEADS, head_dim)
    key = lax.all_gather(triple[:, width : 2 * width], "patch", axis=0, tiled=True)
    value = lax.all_gather(triple[:, 2 * width :], "patch", axis=0, tiled=True)
    key = key.reshape(full, HEADS, head_dim)
    value = value.reshape(full, HEADS, head_dim)
    valid = (jnp.arange(full, dtype=jnp.int32) < count)[None, None, :]

    def score():
        raw = jnp.einsum("qhd,khd->hqk", query, key, preferred_element_type=F32) * scaling
        return jnp.where(valid, raw, MASKED)

    masked = score()
    top = jnp.max(masked, axis=-1, keepdims=True)
    exponent = jnp.exp(masked - top)
    denominator = jnp.sum(exponent, axis=-1, keepdims=True)
    shares_low = (exponent / denominator).astype(BF16)
    lse = top + jnp.log(denominator)
    attended = jnp.einsum("hqk,khd->qhd", shares_low, value, preferred_element_type=F32)

    def backward(grad):
        grad = grad.reshape(seg, HEADS, head_dim)
        shares = jnp.exp(score() - lse)
        share_grad = jnp.einsum("qhd,khd->hqk", grad, value, preferred_element_type=F32)
        dot = jnp.sum(shares * share_grad, axis=-1, keepdims=True)
        score_grad = (shares * (share_grad - dot)).astype(BF16)
        q_grad = jnp.einsum("hqk,khd->qhd", score_grad, key, preferred_element_type=F32) * scaling
        v_all = jnp.einsum("hqk,qhd->khd", shares.astype(BF16), grad, preferred_element_type=F32)
        k_all = jnp.einsum("hqk,qhd->khd", score_grad, query, preferred_element_type=F32) * scaling
        k_grad, v_grad = (
            lax.psum_scatter(
                part.reshape(full, width).astype(BF16), "patch", scatter_dimension=0, tiled=True
            )
            for part in (k_all, v_all)
        )
        return jnp.concatenate([q_grad.reshape(seg, width).astype(BF16), k_grad, v_grad], axis=1)

    return attended.reshape(seg, width).astype(BF16), backward


def exchanged_attention(triple, count, head_dim):
    seg, triple_width = triple.shape
    width = triple_width // 3
    parts = lax.axis_size("patch")
    own = width // parts
    count = count.reshape(1, 1)
    send = triple.reshape(seg, 3, parts, own).transpose(2, 1, 0, 3).reshape(parts, 3 * seg, own)
    qkv = lax.all_to_all(send, "patch", split_axis=0, concat_axis=0, tiled=True)
    out, lse = attend_forward(count, qkv, head_dim)
    back = lax.all_to_all(out.reshape(parts, seg, own), "patch", split_axis=0, concat_axis=0, tiled=True)
    attended = back.transpose(1, 0, 2).reshape(seg, width)

    def backward(grad):
        grads = grad.reshape(seg, parts, own).transpose(1, 0, 2)
        grads = lax.all_to_all(grads, "patch", split_axis=0, concat_axis=0, tiled=True)
        result = attend_backward(count, qkv, grads.reshape(parts * seg, own), lse, head_dim)
        result = lax.all_to_all(result, "patch", split_axis=0, concat_axis=0, tiled=True)
        result = result.reshape(parts, 3, seg, own).transpose(2, 1, 0, 3)
        return result.reshape(seg, 3 * width)

    return attended, backward


def send(values, axis, pairs):
    return lax.ppermute(values, axis, pairs)


def swap(values, axis, bit):
    return lax.ppermute(values, axis, [(i, i ^ bit) for i in range(lax.axis_size(axis))])


def tokens_of_group(values, plan):
    if plan:
        across = swap(values, "var", 2)
        return jnp.concatenate([values, across, swap(values, "var", 1), swap(across, "var", 1)], axis=0)
    return lax.all_gather(values, "var", axis=0, tiled=True)


def slices_of_group(piece_of, plan):
    me = lax.axis_index("var")
    if plan:
        return jnp.concatenate(
            [piece_of(me)] + [swap(piece_of(me ^ bit), "var", bit) for bit in (2, 1, 3)], axis=0
        )
    stacked = jnp.stack([piece_of(v) for v in range(lax.axis_size("var"))])
    moved = lax.all_to_all(stacked, "var", split_axis=0, concat_axis=0, tiled=True)
    return moved.reshape(-1, moved.shape[-1])


def scatter_over_patch(partial, plan):
    parts = lax.axis_size("patch")
    rows, cols = partial.shape[0] // parts, partial.shape[1]
    if not plan:
        return lax.psum_scatter(partial.astype(BF16), "patch", scatter_dimension=0, tiled=True)
    ys, zs = plan
    index = lax.axis_index("patch")
    z, y = index // ys, index % ys
    blocks = partial.reshape(zs, ys, rows, cols)
    away = lax.dynamic_index_in_dim(blocks, 1 - y, 1, keepdims=False).astype(BF16)
    near = lax.dynamic_index_in_dim(blocks, y, 1, keepdims=False)
    held = near + swap(away, "patch", 1).astype(F32)

    def block_of(t):
        return lax.dynamic_index_in_dim(held, jnp.clip(t, 0, zs - 1), 0, keepdims=False)

    up = down = None
    for s in range(1, zs):
        up_out, down_out = block_of(zs + z - s), block_of(z + s - zs)
        if up is not None:
            up_out, down_out = up_out + up.astype(F32), down_out + down.astype(F32)
        up_pairs = [(a * ys + b, (a + 1) * ys + b) for a in range(s) for b in range(ys)]
        down_pairs = [(a * ys + b, (a - 1) * ys + b) for a in range(zs - s, zs) for b in range(ys)]
        up = send(up_out.astype(BF16), "patch", up_pairs)
        down = send(down_out.astype(BF16), "patch", down_pairs)
    return (block_of(z) + up.astype(F32) + down.astype(F32)).astype(BF16)


def gather_over_var(own, plan):
    if not plan:
        return lax.all_gather(own, "var", axis=0)
    me = lax.axis_index("var")
    across = swap(own, "var", 2)
    stacked = jnp.stack([own, swap(own, "var", 1), across, swap(across, "var", 1)])
    return jnp.stack(
        [lax.dynamic_index_in_dim(stacked, me ^ v, 0, keepdims=False) for v in range(lax.axis_size("var"))]
    )


def sum_over_all(values, plan):
    if not plan:
        return lax.psum(values, ("patch", "var"))
    me = lax.axis_index("var")
    half = values.shape[1] // 2
    core, x = me % 2, me // 2

    def part(array, which, size):
        return lax.dynamic_slice_in_dim(array, which * size, size, 1)

    kept = part(values, core, half).astype(F32) + swap(part(values, 1 - core, half), "var", 1).astype(F32)
    quarter = half // 2
    kept = part(kept, x, quarter) + swap(part(kept, 1 - x, quarter).astype(BF16), "var", 2).astype(F32)
    kept = kept.astype(BF16)
    for bit in (1, 2, 4):
        kept = (kept.astype(F32) + swap(kept, "patch", bit).astype(F32)).astype(BF16)
    pieces = gather_over_var(kept, plan)
    return jnp.concatenate([pieces[(v % 2) * 2 + v // 2] for v in range(4)], axis=1)


def small_sum_over_all(values, plan):
    if not plan:
        return lax.psum(values, ("patch", "var"))
    for axis, bit in (("var", 1), ("var", 2), ("patch", 1), ("patch", 2), ("patch", 4)):
        values = values + swap(values, axis, bit)
    return values


def local(
    input_field,
    counts,
    var_ids,
    patch_weight,
    var_embed,
    agg_query,
    query_proj,
    key_proj,
    value_proj,
    agg_out,
    norm_one,
    trunk_qkv,
    trunk_out,
    norm_two,
    mlp_in,
    mlp_out,
    cotangent,
):
    patches, group = lax.axis_size("patch"), lax.axis_size("var")
    plan = (2, 4) if (patches, group) == (8, 4) else None
    var_index = lax.axis_index("var")
    patch_index = lax.axis_index("patch")
    all_rows, seg, var_local, pixels = input_field.shape
    width = agg_out.shape[0]
    head_dim = width // HEADS
    hidden = mlp_in.shape[1]
    scaling = 1.0 / math.sqrt(head_dim)

    turned = input_field.transpose(0, 2, 3, 1).reshape(all_rows, var_local * pixels, seg)
    own_field = lax.all_to_all(turned, "var", split_axis=0, concat_axis=1, tiled=True)
    own_field = own_field.reshape(VARS * pixels, seg)
    own_ids = lax.dynamic_slice_in_dim(var_ids, var_index, 1, 0)
    own_count = lax.dynamic_slice_in_dim(counts, var_index, 1, 0)
    positions = patch_index * seg + jnp.arange(seg, dtype=jnp.int32)
    valid_rows = (positions < own_count).astype(F32)[:, None]
    out_grad = cotangent.reshape(seg, width).astype(F32) * valid_rows
    out_grad_low = out_grad.astype(BF16)
    out_grad_group = tokens_of_group(out_grad_low, plan)

    weight_rows = patch_weight.reshape(VARS * pixels, width)
    agg_q = mm(agg_query[None], query_proj)[0]
    in_head = jnp.arange(width, dtype=jnp.int32)[:, None] // head_dim == jnp.arange(HEADS)[None, :]
    head_query = jnp.where(in_head, agg_q[:, None] * scaling, 0.0)
    key_query = mm(key_proj, jnp.concatenate(split_high_low(head_query), axis=1))
    key_query = key_query[:, :HEADS] + key_query[:, HEADS:]
    key_query_parts = jnp.concatenate(split_high_low(key_query), axis=1)
    score_weight = mm(key_query_parts, weight_rows, (((0,), (1,)), ((), ())))
    score_weight = score_weight[:HEADS] + score_weight[HEADS:]
    score_embed = mm(key_query_parts, var_embed, (((0,), (1,)), ((), ())))
    score_embed = (score_embed[:HEADS] + score_embed[HEADS:]).reshape(HEADS * VARS, 1)
    same_var = (jnp.arange(VARS)[:, None] == jnp.arange(VARS * pixels)[None, :] // pixels)[None]
    spread = jnp.where(same_var, score_weight[:, None, :], 0.0).astype(BF16)
    spread = spread.reshape(HEADS * VARS, VARS * pixels)
    vw = mm(weight_rows, value_proj).astype(BF16)
    ve = mm(var_embed, value_proj).astype(BF16)
    vwt = mm(value_proj, weight_rows, (((0,), (1,)), ((), ()))).astype(BF16)
    vet = mm(value_proj, var_embed, (((0,), (1,)), ((), ()))).astype(BF16)

    x_own, shares, mixed_low = front_forward(own_ids, own_field, spread, score_embed, vwt, vet)

    mixed_group = tokens_of_group(mixed_low, plan)
    front_out = mm(mixed_low, agg_out) * valid_rows
    normed_one, norm_one_pull = jax.vjp(layer_norm, front_out, norm_one.astype(F32))
    normed_one_low = normed_one.astype(BF16)
    triple = mm(normed_one_low, trunk_qkv).astype(BF16)
    normed_one_group = tokens_of_group(normed_one_low, plan)
    attention = exchanged_attention if HEADS % patches == 0 else gathered_attention
    attended, attention_pull = attention(triple, own_count, head_dim)
    attended_group = tokens_of_group(attended, plan)
    after_attn = front_out + mm(attended, trunk_out)
    normed_two, norm_two_pull = jax.vjp(layer_norm, after_attn, norm_two.astype(F32))
    normed_two_low = normed_two.astype(BF16)
    normed_two_group = tokens_of_group(normed_two_low, plan)
    inner = mm(normed_two_low, mlp_in)
    active, gelu_pull = jax.vjp(gelu_exact, inner)
    active_low = active.astype(BF16)
    result = after_attn + mm(active_low, mlp_out)
    block_out = (result * valid_rows).astype(BF16)[None]

    def column_slice(values):
        size = values.shape[1] // group
        return lambda v: lax.dynamic_slice_in_dim(values, v * size, size, 1)

    def hidden_slice(values):
        size = hidden // (patches * group)

        def piece(v):
            return jnp.concatenate(
                [lax.dynamic_slice_in_dim(values, (p * group + v) * size, size, 1) for p in range(patches)], axis=1
            )

        return piece

    active_group = slices_of_group(hidden_slice(active_low), plan)
    inner_grad = gelu_pull(mm(out_grad_low, mlp_out, NT))[0].astype(BF16)
    inner_grad_group = slices_of_group(column_slice(inner_grad), plan)
    normed_two_grad = mm(inner_grad, mlp_in, NT)
    after_ln_grad, norm_two_grad = norm_two_pull(normed_two_grad)
    after_grad = out_grad + after_ln_grad
    branch_low = after_grad.astype(BF16)
    branch_group = slices_of_group(column_slice(branch_low), plan)
    attended_grad = mm(branch_low, trunk_out, NT).astype(BF16)
    mlp_out_own = scatter_over_patch(mm(active_group, out_grad_group, TN), plan)
    mlp_in_own = scatter_over_patch(mm(normed_two_group, inner_grad_group, TN), plan)
    triple_grad = attention_pull(attended_grad)
    triple_grad_group = slices_of_group(column_slice(triple_grad), plan)
    normed_one_grad = mm(triple_grad, trunk_qkv, NT)
    front_ln_grad, norm_one_grad = norm_one_pull(normed_one_grad)
    agg_grad = ((after_grad + front_ln_grad) * valid_rows).astype(BF16)
    agg_grad_group = slices_of_group(column_slice(agg_grad), plan)
    mixed_grad = mm(agg_grad, agg_out, NT).astype(BF16)

    field_grad, m_part, me_part, s_part, se_part = front_backward(
        own_ids, x_own, shares, mixed_grad, vw, ve, spread
    )
    field_grad = lax.all_to_all(
        field_grad.reshape(1, VARS * pixels, seg), "var", split_axis=1, concat_axis=0, tiled=True
    )
    field_grad = field_grad.reshape(all_rows, var_local, pixels, seg).transpose(0, 3, 1, 2)

    square = jnp.concatenate(
        [
            mm(attended_group, branch_group, TN),
            mm(mixed_group, agg_grad_group, TN),
            mm(normed_one_group, triple_grad_group, TN),
        ],
        axis=1,
    )
    square_own = scatter_over_patch(square, plan)

    small = jnp.concatenate(
        [
            s_part,
            jnp.pad(se_part.reshape(HEADS, VARS), ((0, 0), (0, 2 * width - VARS * pixels - VARS))),
        ],
        axis=1,
    )
    norms = jnp.concatenate([norm_one_grad, norm_two_grad])[None]
    small = small_sum_over_all(jnp.concatenate([small, norms], axis=0), plan)
    s_all = small[:HEADS, : VARS * pixels]
    se_all = small[:HEADS, VARS * pixels : VARS * pixels + VARS]
    norm_sums = small[HEADS]
    m_all = sum_over_all(jnp.concatenate([m_part, me_part], axis=0), plan)
    m_sum, me_sum = m_all[: VARS * pixels], m_all[VARS * pixels :]

    own_width = width // patches
    start = patch_index * own_width

    def own_cols(values):
        return lax.dynamic_slice_in_dim(values, start, own_width, 1)

    def own_rows(values):
        return lax.dynamic_slice_in_dim(values, start, own_width, 0)

    value_proj_grad = mm(own_cols(weight_rows), m_sum, TN) + mm(own_cols(var_embed), me_sum, TN)
    value_rows = own_rows(value_proj)
    key_query_rows = own_rows(key_query)
    patch_grad = mm(m_sum, value_rows, NT) + mm(
        s_all, key_query_rows, (((0,), (1,)), ((), ())), precision=HIGHEST
    )
    patch_grad = patch_grad.reshape(VARS, pixels, own_width)
    embed_grad = mm(me_sum, value_rows, NT) + mm(
        se_all, key_query_rows, (((0,), (1,)), ((), ())), precision=HIGHEST
    )
    s_parts = jnp.concatenate(split_high_low(s_all), axis=0)
    se_parts = jnp.concatenate(split_high_low(se_all), axis=0)
    key_sum = mm(s_parts, weight_rows) + mm(se_parts, var_embed)
    key_sum = (key_sum[:HEADS] + key_sum[HEADS:]) * scaling
    head_rows = jnp.where(in_head.T, agg_q[None, :], 0.0)
    key_proj_grad = mm(own_cols(key_sum), head_rows, TN, precision=HIGHEST)
    crossed = mm(jnp.concatenate(split_high_low(key_sum), axis=0), key_proj)
    crossed = crossed[:HEADS] + crossed[HEADS:]
    aggq_grad = jnp.sum(jnp.where(in_head.T, crossed, 0.0), axis=0)
    own_query = lax.dynamic_slice_in_dim(agg_query, start, own_width, 0).astype(F32)
    query_proj_grad = own_query[:, None] * aggq_grad[None, :]
    agg_query_grad = jnp.sum(own_rows(query_proj).astype(F32) * aggq_grad[None, :], axis=1)

    def joined(values):
        pieces = gather_over_var(values, plan)
        return jnp.concatenate([pieces[v] for v in range(group)], axis=1).astype(F32)

    mlp_out_grad = gather_over_var(mlp_out_own, plan).reshape(hidden // patches, width).astype(F32)
    mlp_in_grad = joined(mlp_in_own)
    part = width // group
    trunk_out_grad = joined(square_own[:, :part])
    agg_out_grad = joined(square_own[:, part : 2 * part])
    trunk_qkv_grad = joined(square_own[:, 2 * part :])
    norm_one_grad = lax.dynamic_slice_in_dim(norm_sums, start, own_width, 0)
    norm_two_grad = lax.dynamic_slice_in_dim(norm_sums, width + start, own_width, 0)
    return (
        block_out,
        field_grad,
        patch_grad,
        embed_grad,
        agg_query_grad,
        query_proj_grad,
        key_proj_grad,
        value_proj_grad,
        agg_out_grad,
        norm_one_grad,
        trunk_qkv_grad,
        trunk_out_grad,
        norm_two_grad,
        mlp_in_grad,
        mlp_out_grad,
    )


def solution(mesh):
    whole = P()
    placed = (P(None, "patch", "var", None),) + (whole,) * 15 + (P("var", "patch", None),)
    rows = P("patch", None)
    return jax.shard_map(
        local,
        mesh=mesh,
        in_specs=placed,
        out_specs=(
            P("var", "patch", None),
            P(None, "patch", "var", None),
            P(None, None, "patch"),
            P(None, "patch"),
            P("patch"),
            rows,
            rows,
            rows,
            rows,
            P("patch"),
            rows,
            rows,
            P("patch"),
            rows,
            rows,
        ),
        check_vma=False,
    )
```

time: 1850 us -> 458 us (0.25)
  waiting for transfers between devices: 1000 us -> 100 us
  local copies, waits for them, and re-layouts: 335 us -> 70.8 us
  matrix products: 277 us -> 69.8 us
  starting transfers between devices: 12.8 us -> 125 us
  other arithmetic: 154 us -> 44.4 us
  blocking collectives: 40.8 us -> 0 us
  Pallas kernels: 0 us -> 35.3 us
    reduce_scatter x8 -> x0, waiting for transfers between devices: 698 us -> none  [the longest x1 153 us: local(): lax.psum_scatter(mlp_in_grad.astype(jnp.bfloat16), 'patch', scatter_dimen...]
    dot_general x36 -> x33, matrix products: 277 us -> 69.8 us  [mm(): lax.dot_general(a, b, dims, precision=precision, preferred_element_type=F32)]
    unnamed x20 -> x0, waiting for transfers between devices: 119 us -> none
    ppermute x0 -> x79, starting transfers between devices: none -> 95.7 us  [the longest x61 63 us: swap(): lax.ppermute(values, axis, [(i, i ^ bit) for i in range(lax.axis_size(axi...]
    all_gather x3 -> x0, waiting for transfers between devices: 92.1 us -> none  [the longest x1 46.7 us: local(): lax.all_gather(key_low, 'patch', axis=1, tiled=True)]
    reshape x4 -> x8, local copies, waits for them, and re-layouts: 105 us -> 15.5 us  [the longest x1 8.16 us: scatter_over_patch(): blocks = partial.reshape(zs, ys, rows, cols)]
    convert_element_type x7, local copies, waits for them, and re-layouts: 88.6 us -> 4 us  [the longest x3 1.81 us: scatter_over_patch(): up = send(up_out.astype(BF16), 'patch', up_pairs)]
    ppermute x0 -> x79, waiting for transfers between devices: none -> 84.5 us  [the longest x61 84.4 us: swap(): lax.ppermute(values, axis, [(i, i ^ bit) for i in range(lax.axis_size(axi...]
  transfers between devices with their start and end apart: 19 -> 85, of which waited for: 15 -> 14; matrix products, arithmetic and copies ran while one was open for 16% -> 36% of each run, Pallas kernels for 0% -> 6%
where the time goes in v1:
time: 458 us; the launch traced here: 449 us
  starting transfers between devices  125 us (27%)
  waiting for transfers between devices  100 us (22%)
  local copies, waits for them, and re-layouts  70.8 us (15%)
  matrix products  69.8 us (15%)
  other arithmetic  44.4 us (10%)
  Pallas kernels  35.3 us (8%)
    ppermute x61, waiting for transfers between devices, swap(): lax.ppermute(values, axis, [(i, i ^ bit) for i in range(lax.axis_size(axi...  84.4 us
    dot_general x33, matrix products, mm(): lax.dot_general(a, b, dims, precision=precision, preferred_element_type=F32)  69.8 us
    ppermute x61, starting transfers between devices, swap(): lax.ppermute(values, axis, [(i, i ^ bit) for i in range(lax.axis_size(axi...  63 us
    ppermute x18, starting transfers between devices, send(): return lax.ppermute(values, axis, pairs)  32.8 us
    unnamed x115, local copies, waits for them, and re-layouts  25 us
    all_to_all x1, waiting for transfers between devices, exchanged_attention(): qkv = lax.all_to_all(send, 'patch', split_axis=0, concat_axis=0, tiled=True)  15.9 us
    dynamic_slice x2, local copies, waits for them, and re-layouts, scatter_over_patch(): near = lax.dynamic_index_in_dim(blocks, y, 1, keepdims=False)  13.4 us
    pallas_call x1, Pallas kernels, attend_backward(): pl.pallas_call(functools.partial(attend_backward_kernel, head_dim, block)...  11 us
  transfers between devices with their start and end apart: 85, of which 14 were waited for; matrix products, arithmetic and copies ran while one was open for 36% of the time, Pallas kernels for 6%

profile of v1, /device:TPU:1, one launch (start us, length us, event | category | flops | bytes accessed | tf_op | source)
XLA Modules:
  0.0 448.5 jit_solution(16547475735510388570)
XLA Ops:
  0.7 4.4 all-to-all-start
  5.9 2.1 fusion.189
  10.2 3.1 convolution_convert_fusion.2.vwt_ref
  19.8 6.5 %front_forward.1 = (bf16[768,128]{1,0:T(8,128)(2,1)}, f32[768,128]{1,0:T(8,128)}, bf16[128,1024]{1,0:T(8,128)(2,1)}) custom-call(s32[1,48]{1,0:T(1,128)} %constant_dynamic-slice_fusion.28.ids_ref, bf16[768,128]{1,0:T(8,128)(2,1)} %bitcast.289, bf16[768,768]{1,0:T(8,128)(2,1)} %bitcast.263, f32[768,1]{1,0:T(8,128)} %reshape.311.bias_ref, ...), custom_call_target="tpu_custom_call" | custom-call | tf_op jit(solution)/shard_map/front_forward/pallas_call | solution.py:74
  26.3 2.2 fusion.187
  29.6 3.9 fusion.10
  34.8 6.1 %all-to-all-start.1 = ((bf16[8,384,128]{2,1,0:T(8,128)(2,1)}), bf16[8,384,128]{2,1,0:T(8,128)(2,1)S(1)}, u32[]{:S(2)}, u32[]{:S(2)}) async-start(bf16[8,384,128]{2,1,0:T(8,128)(2,1)} %bitcast.272), calls=%async_computation.1 | async-start | bytes 1572864 | tf_op jit(solution)/shard_map/all_to_all | solution.py:347
  45.0 15.9 %all-to-all-done.1.qkv_ref = bf16[8,384,128]{2,1,0:T(8,128)(2,1)S(1)} async-done(((bf16[8,384,128]{2,1,0:T(8,128)(2,1)}), bf16[8,384,128]{2,1,0:T(8,128)(2,1)S(1)}, u32[]{:S(2)}, u32[]{:S(2)}) %all-to-all-start.1) | async-done | bytes 786464 | tf_op jit(solution)/shard_map/all_to_all | solution.py:347
  61.8 10.2 %attend_forward.1 = (bf16[1024,128]{1,0:T(8,128)(2,1)}, f32[2,1024]{1,0:T(2,128)}) custom-call(s32[1,1]{1,0:T(1,128)} %bitcast.8.count_ref, bf16[8,384,128]{2,1,0:T(8,128)(2,1)} %copy-done.13), custom_call_target="tpu_custom_call" | custom-call | tf_op jit(solution)/shard_map/attend_forward/pallas_call | solution.py:217
  72.0 1.8 copy.77
  73.8 4.5 %all-to-all-start.2 = ((bf16[8,128,128]{1,2,0:T(8,128)(2,1)}), bf16[8,128,128]{1,2,0:T(8,128)(2,1)S(1)}, u32[]{:S(2)}, u32[]{:S(2)}) async-start(bf16[8,128,128]{1,2,0:T(8,128)(2,1)} %copy.77), calls=%async_computation.2 | async-start | bytes 524288 | tf_op jit(solution)/shard_map/all_to_all | solution.py:349
  78.3 4.3 convolution_convert_fusion.1.vw_ref
  85.8 2.2 fusion.188
  90.5 5.1 %fusion.190 = f32[128,4096]{1,0:T(8,128)S(1)} fusion(bf16[128,1024]{1,0:T(8,128)(2,1)} %multiply_convert_fusion.2, bf16[1024,4096]{1,0:T(8,128)(2,1)} %param.31), kind=kOutput, calls=%fused_computation.402 | convolution fusion | flops 1073741824 | bytes 10747904 | tf_op jit(solution)/shard_map/dot_general | solution.py:24
  95.6 8.2 %add_convert_fusion = (bf16[128,4096]{1,0:T(8,128)(2,1)S(1)}, f32[128,4096]{1,0:T(8,128)S(1)}) fusion(f32[128,4096]{1,0:T(8,128)S(1)} %fusion.190, bf16[128,1024]{1,0:T(8,128)(2,1)} %fusion.88, bf16[4096,1024]{1,0:T(8,128)(2,1)S(1)} %bitcast.262), kind=kOutput, calls=%fused_computation.10 | convolution fusion | flops 1111490560 | bytes 13893632 | tf_op jit(solution)/shard_map/dot_general | solution.py:24
  104.8 3.2 multiply_reduce_fusion.1
  113.7 2.5 collective-permute-start.65
  118.8 4.4 all-to-all-start.3
  123.1 2.2 constant_dynamic-slice_fusion.7
  129.2 2.7 fusion.59
  131.9 2.0 copy-done.21
  135.1 11.0 %attend_backward.1 = bf16[8,384,128]{2,1,0:T(8,128)(2,1)} custom-call(s32[1,1]{1,0:T(1,128)} %bitcast.8.count_ref, bf16[8,384,128]{2,1,0:T(8,128)(2,1)} %copy-done.13, bf16[1024,128]{1,0:T(8,128)(2,1)} %bitcast.17.grad_ref, f32[2,1024]{1,0:T(2,128)} %get-tuple-element.29.lse_ref), custom_call_target="tpu_custom_call" | custom-call | tf_op jit(solution)/shard_map/attend_backward/pallas_call | solution.py:284
  146.1 5.4 %all-to-all-start.4 = ((bf16[8,384,128]{2,1,0:T(8,128)(2,1)}), bf16[8,384,128]{2,1,0:T(8,128)(2,1)}, u32[]{:S(2)}, u32[]{:S(2)}) async-start(bf16[8,384,128]{2,1,0:T(8,128)(2,1)} %attend_backward.1), calls=%async_computation.4 | async-start | bytes 1572864 | tf_op jit(solution)/shard_map/all_to_all | solution.py:356
  155.9 2.8 fusion.44
  158.9 2.5 collective-permute-done.18
  163.6 5.4 %fusion.17 = bf16[1,128,1024]{2,1,0:T(8,128)(2,1)} fusion(f32[128,1024]{1,0:T(8,128)S(1)} %get-tuple-element.151, bf16[128,4096]{1,0:T(8,128)(2,1)S(1)} %copy-done.3, bf16[4096,1024]{1,0:T(8,128)(2,1)} %param.32, f32[128]{0:T(128)S(1)} %compare_convert_fusion), kind=kOutput, calls=%fused_computation.46 | convolution fusion | flops 1074135040 | bytes 10224128 | tf_op jit(solution)/shard_map/dot_general | solution.py:24
  172.0 13.2 %collective-permute-done.69 = bf16[4,128,1024]{2,1,0:T(8,128)(2,1)S(1)} collective-permute-done((bf16[4,128,1024]{2,1,0:T(8,128)(2,1)}, bf16[4,128,1024]{2,1,0:T(8,128)(2,1)S(1)}, u32[]{:S(2)}, u32[]{:S(2)}) %collective-permute-start.69) | collective-permute-done | bytes 1048608 | tf_op jit(solution)/shard_map/ppermute | solution.py:368
  186.6 3.1 collective-permute-start.70
  191.0 16.7 %collective-permute-done.53 = bf16[4,128,1024]{2,1,0:T(8,128)(2,1)S(1)} collective-permute-done((bf16[4,128,1024]{2,1,0:T(8,128)(2,1)S(1)}, bf16[4,128,1024]{2,1,0:T(8,128)(2,1)S(1)}, u32[]{:S(2)}, u32[]{:S(2)}) %collective-permute-start.53) | collective-permute-done | bytes 1048608 | tf_op jit(solution)/shard_map/ppermute | solution.py:368
  210.3 3.8 collective-permute-start.54
  214.9 2.2 collective-permute-start.71
  218.6 5.2 %multiply_reduce_fusion.2 = (f32[1024]{0:T(1024)S(1)}, f32[128]{0:T(128)S(1)}, f32[128,1024]{1,0:T(8,128)S(1)}) fusion(f32[128,1024]{1,0:T(8,128)S(1)} %get-tuple-element.149, f32[128]{0:T(128)S(1)} %fusion.167, f32[128]{0:T(128)S(1)} %broadcast_multiply_fusion.3, f32[1024]{0:T(1024)S(1)} %convert_element_type.357, bf16[128,3072]{0,1:T(8,128)(2,1)S(1)} %bitcast.270, ...), kind=kOutput, calls=%fused_computation.173 | convolution fusion | flops 806222720 | bytes 8136192 | tf_op jit(solution)/shard_map/dot_general | solution.py:24
  226.9 7.6 %front_backward.1 = (bf16[768,128]{1,0:T(8,128)(2,1)}, bf16[768,1024]{1,0:T(8,128)(2,1)}, bf16[48,1024]{1,0:T(8,128)(2,1)}, f32[16,768]{1,0:T(8,128)}, f32[768,1]{1,0:T(8,128)}) custom-call(s32[1,48]{1,0:T(1,128)} %constant_dynamic-slice_fusion.28.ids_ref, bf16[768,128]{1,0:T(8,128)(2,1)} %get-tuple-element.27.x_ref, f32[768,128]{1,0:T(8,128)} %get-tuple-element.28.p_ref, ...), custom_call_target="tpu_custom_call" | custom-call | tf_op jit(solution)/shard_map/front_backward/pallas_call | solution.py:159
  239.8 2.5 reduce.1
  243.9 4.7 %all-to-all-start.5 = ((bf16[4,2,12288]{2,1,0:T(2,128)(2,1)}), bf16[4,2,12288]{2,1,0:T(2,128)(2,1)}, u32[]{:S(2)}, u32[]{:S(2)}) async-start(bf16[4,2,12288]{2,1,0:T(2,128)(2,1)} %reshape.313), calls=%async_computation.5 | async-start | bytes 393216 | tf_op jit(solution)/shard_map/all_to_all | solution.py:572
  249.1 1.9 fusion.97
  252.8 2.3 fusion.92
  268.3 2.5 collective-permute-start.55
  272.1 2.2 collective-permute-start.72
  274.3 2.6 fusion.36
  277.0 2.8 pad_maximum_fusion
  279.8 8.2 %reshape.304 = f32[4,2,128,1280]{2,1,0,3:T(2,128)} reshape(f32[1024,1280]{0,1:T(8,128)} %pad_maximum_fusion) | data formatting | bytes 10485760 | tf_op jit(solution)/shard_map/reshape | solution.py:397
  288.0 7.0 %constant_dynamic-slice_fusion.11 = f32[4,1,128,1280]{2,1,0,3:T(1,128)} fusion(f32[4,2,128,1280]{2,1,0,3:T(2,128)} %reshape.304, s32[]{:T(128)S(6)} %select_n.328), kind=kLoop, calls=%fused_computation.320 | loop fusion | bytes 5242884 | tf_op jit(solution)/shard_map/jit(dynamic_index_in_dim)/dynamic_slice | solution.py:399
  296.4 2.3 fusion.98
  300.1 1.9 fusion.90
  304.3 3.8 constant_dynamic-slice_fusion.10
  308.1 6.4 %copy.81 = f32[4,1,128,1280]{3,2,0,1:T(8,128)} copy(f32[4,1,128,1280]{2,1,0,3:T(1,128)} %constant_dynamic-slice_fusion.11) | data formatting | bytes 5242880 | tf_op jit(solution)/shard_map/jit(dynamic_index_in_dim)/dynamic_slice | solution.py:399
  314.5 4.9 %copy.84 = bf16[4,1,128,1280]{3,2,0,1:T(8,128)(2,1)S(1)} copy(bf16[4,1,128,1280]{2,1,0,3:T(2,128)(2,1)} %constant_dynamic-slice_fusion.10) | data formatting | bytes 2621440
  321.8 2.1 collective-permute-start.11
  325.1 2.4 collective-permute-done.11
  327.5 3.1 collective-permute-start.56
  332.1 4.4 collective-permute-start.12
  337.9 7.9 %collective-permute-done.12 = f32[17,2048]{1,0:T(8,128)S(1)} collective-permute-done((f32[17,2048]{1,0:T(8,128)S(1)}, f32[17,2048]{1,0:T(8,128)S(1)}, u32[]{:S(2)}, u32[]{:S(2)}) %collective-permute-start.12) | collective-permute-done | bytes 139296 | tf_op jit(solution)/shard_map/ppermute | solution.py:368
  348.4 2.4 broadcast_multiply_fusion
  351.3 6.6 %collective-permute-start.76 = (bf16[128,1024]{1,0:T(8,128)(2,1)S(1)}, bf16[128,1024]{1,0:T(8,128)(2,1)S(1)}, u32[]{:S(2)}, u32[]{:S(2)}) collective-permute-start(bf16[128,1024]{1,0:T(8,128)(2,1)S(1)} %fusion.94), channel_id=1, source_target_pairs={{0,1},{1,0},{2,3},{3,2},{4,5},{5,4},{6,7},{7,6},{8,9},{9,8},{10,11... | collective-permute-start | bytes 786440 | tf_op jit(solution)/shard_map/ppermute | solution.py:368
  366.4 9.7 %collective-permute-done.1 = bf16[816,256]{1,0:T(8,128)(2,1)S(1)} collective-permute-done((bf16[816,256]{1,0:T(8,128)(2,1)S(1)}, bf16[816,256]{1,0:T(8,128)(2,1)S(1)}, u32[]{:S(2)}, u32[]{:S(2)}) %collective-permute-start.1) | collective-permute-done | bytes 417824 | tf_op jit(solution)/shard_map/ppermute | solution.py:368
  381.3 5.3 %collective-permute-done.2 = bf16[816,256]{1,0:T(8,128)(2,1)S(1)} collective-permute-done((bf16[816,256]{1,0:T(8,128)(2,1)S(1)}, bf16[816,256]{1,0:T(8,128)(2,1)S(1)}, u32[]{:S(2)}, u32[]{:S(2)}) %collective-permute-start.2) | collective-permute-done | bytes 417824 | tf_op jit(solution)/shard_map/ppermute | solution.py:368
  387.8 8.4 %collective-permute-done.3 = bf16[816,256]{1,0:T(8,128)(2,1)S(1)} collective-permute-done((bf16[816,256]{1,0:T(8,128)(2,1)S(1)}, bf16[816,256]{1,0:T(8,128)(2,1)S(1)}, u32[]{:S(2)}, u32[]{:S(2)}) %collective-permute-start.3) | collective-permute-done | bytes 417824 | tf_op jit(solution)/shard_map/ppermute | solution.py:368
  396.5 2.2 collective-permute-start.34
  400.5 14.4 %collective-permute-done.4 = bf16[816,256]{1,0:T(8,128)(2,1)S(1)} collective-permute-done((bf16[816,256]{1,0:T(8,128)(2,1)S(1)}, bf16[816,256]{1,0:T(8,128)(2,1)S(1)}, u32[]{:S(2)}, u32[]{:S(2)}) %collective-permute-start.4) | collective-permute-done | bytes 417824 | tf_op jit(solution)/shard_map/ppermute | solution.py:368
  418.4 6.7 %collective-permute-start.5 = (bf16[816,256]{1,0:T(8,128)(2,1)S(1)}, bf16[816,256]{1,0:T(8,128)(2,1)S(1)}, u32[]{:S(2)}, u32[]{:S(2)}) collective-permute-start(bf16[816,256]{1,0:T(8,128)(2,1)S(1)} %add_convert_fusion.1), channel_id=1, source_target_pairs={{0,1},{1,0},{2,3},{3,2},{4,5},{5,4},{6,7},{7,6},{8,9},{9,8},{10,11... | collective-permute-start | bytes 1253384 | tf_op jit(solution)/shard_map/ppermute | solution.py:368
  426.5 4.2 collective-permute-start.46
  434.2 2.7 collective-permute-done.42
  443.1 2.2 convolution_add_fusion.2
  (378 shorter events, 128.8 us)
Async XLA Ops:
  0.7 18.5 %all-to-all-start = ((bf16[4,192,128]{2,1,0:T(8,128)(2,1)}), bf16[4,192,128]{2,1,0:T(8,128)(2,1)S(1)}, u32[]{:S(2)}, u32[]{:S(2)}) async-start(bf16[4,192,128]{2,1,0:T(8,128)(2,1)} %bitcast.304), calls=%async_computation | async-start | bytes 393216 | tf_op jit(solution)/shard_map/all_to_all | solution.py:486
  34.8 26.1 %all-to-all-start.1 = ((bf16[8,384,128]{2,1,0:T(8,128)(2,1)}), bf16[8,384,128]{2,1,0:T(8,128)(2,1)S(1)}, u32[]{:S(2)}, u32[]{:S(2)}) async-start(bf16[8,384,128]{2,1,0:T(8,128)(2,1)} %bitcast.272), calls=%async_computation.1 | async-start | bytes 1572864 | tf_op jit(solution)/shard_map/all_to_all | solution.py:347
  42.6 42.4 %collective-permute-start.66 = (bf16[128,1024]{1,0:T(8,128)(2,1)}, bf16[128,1024]{1,0:T(8,128)(2,1)}, u32[]{:S(2)}, u32[]{:S(2)}) collective-permute-start(bf16[128,1024]{1,0:T(8,128)(2,1)} %fusion.88), channel_id=1, source_target_pairs={{0,2},{1,3},{2,0},{3,1},{4,6},{5,7},{6,4},{7,5},{8,10},{9,11},{10,... | collective-permute-start | bytes 786440 | tf_op jit(solution)/shard_map/ppermute | solution.py:368
  44.0 72.2 %collective-permute-start.67 = (bf16[128,1024]{1,0:T(8,128)(2,1)}, bf16[128,1024]{1,0:T(8,128)(2,1)}, u32[]{:S(2)}, u32[]{:S(2)}) collective-permute-start(bf16[128,1024]{1,0:T(8,128)(2,1)} %fusion.88), channel_id=1, source_target_pairs={{0,1},{1,0},{2,3},{3,2},{4,5},{5,4},{6,7},{7,6},{8,9},{9,8},{10,11... | collective-permute-start | bytes 786440 | tf_op jit(solution)/shard_map/ppermute | solution.py:368
  73.8 12.1 %all-to-all-start.2 = ((bf16[8,128,128]{1,2,0:T(8,128)(2,1)}), bf16[8,128,128]{1,2,0:T(8,128)(2,1)S(1)}, u32[]{:S(2)}, u32[]{:S(2)}) async-start(bf16[8,128,128]{1,2,0:T(8,128)(2,1)} %copy.77), calls=%async_computation.2 | async-start | bytes 524288 | tf_op jit(solution)/shard_map/all_to_all | solution.py:349
  85.1 41.0 %collective-permute-start.68 = (bf16[128,1024]{1,0:T(8,128)(2,1)}, bf16[128,1024]{1,0:T(8,128)(2,1)}, u32[]{:S(2)}, u32[]{:S(2)}) collective-permute-start(bf16[128,1024]{1,0:T(8,128)(2,1)} %collective-permute-done.66), channel_id=1, source_target_pairs={{0,1},{1,0},{2,3},{3,2},{4,5},{5,4},{6,7},{7,6},{8,9},{9,8},{10,11... | collective-permute-start | bytes 786440 | tf_op jit(solution)/shard_map/ppermute | solution.py:368
  89.2 37.5 %collective-permute-start.47 = (bf16[128,1024]{1,0:T(8,128)(2,1)}, bf16[128,1024]{1,0:T(8,128)(2,1)}, u32[]{:S(2)}, u32[]{:S(2)}) collective-permute-start(bf16[128,1024]{1,0:T(8,128)(2,1)} %multiply_convert_fusion.2), channel_id=1, source_target_pairs={{0,2},{1,3},{2,0},{3,1},{4,6},{5,7},{6,4},{7,5},{8,10},{9,11},{10,... | collective-permute-start | bytes 786440 | tf_op jit(solution)/shard_map/ppermute | solution.py:368
  113.7 13.6 %collective-permute-start.65 = (bf16[128,1024]{1,0:T(8,128)(2,1)}, bf16[128,1024]{1,0:T(8,128)(2,1)}, u32[]{:S(2)}, u32[]{:S(2)}) collective-permute-start(bf16[128,1024]{1,0:T(8,128)(2,1)} %get-tuple-element.75), channel_id=1, source_target_pairs={{0,3},{1,2},{2,1},{3,0},{4,7},{5,6},{6,5},{7,4},{8,11},{9,10},{10,... | collective-permute-start | bytes 786440 | tf_op jit(solution)/shard_map/ppermute | solution.py:368
  116.1 11.6 %collective-permute-start.64 = (bf16[128,1024]{1,0:T(8,128)(2,1)}, bf16[128,1024]{1,0:T(8,128)(2,1)}, u32[]{:S(2)}, u32[]{:S(2)}) collective-permute-start(bf16[128,1024]{1,0:T(8,128)(2,1)} %get-tuple-element.76), channel_id=1, source_target_pairs={{0,1},{1,0},{2,3},{3,2},{4,5},{5,4},{6,7},{7,6},{8,9},{9,8},{10,11... | collective-permute-start | bytes 786440 | tf_op jit(solution)/shard_map/ppermute | solution.py:368
  116.3 12.7 %collective-permute-start.63 = (bf16[128,1024]{1,0:T(8,128)(2,1)}, bf16[128,1024]{1,0:T(8,128)(2,1)}, u32[]{:S(2)}, u32[]{:S(2)}) collective-permute-start(bf16[128,1024]{1,0:T(8,128)(2,1)} %get-tuple-element.77), channel_id=1, source_target_pairs={{0,2},{1,3},{2,0},{3,1},{4,6},{5,7},{6,4},{7,5},{8,10},{9,11},{10,... | collective-permute-start | bytes 786440 | tf_op jit(solution)/shard_map/ppermute | solution.py:368
  118.8 16.3 %all-to-all-start.3 = ((bf16[8,128,128]{2,1,0:T(8,128)(2,1)}), bf16[8,128,128]{2,1,0:T(8,128)(2,1)}, u32[]{:S(2)}, u32[]{:S(2)}) async-start(bf16[8,128,128]{2,1,0:T(8,128)(2,1)} %bitcast.286), calls=%async_computation.3 | async-start | bytes 524288 | tf_op jit(solution)/shard_map/all_to_all | solution.py:354
  126.0 25.5 %collective-permute-start.48 = (bf16[128,1024]{1,0:T(8,128)(2,1)}, bf16[128,1024]{1,0:T(8,128)(2,1)}, u32[]{:S(2)}, u32[]{:S(2)}) collective-permute-start(bf16[128,1024]{1,0:T(8,128)(2,1)} %multiply_convert_fusion.2), channel_id=1, source_target_pairs={{0,1},{1,0},{2,3},{3,2},{4,5},{5,4},{6,7},{7,6},{8,9},{9,8},{10,11... | collective-permute-start | bytes 786440 | tf_op jit(solution)/shard_map/ppermute | solution.py:368
  126.7 25.6 %collective-permute-start.52 = (bf16[128,1024]{1,0:T(8,128)(2,1)}, bf16[128,1024]{1,0:T(8,128)(2,1)}, u32[]{:S(2)}, u32[]{:S(2)}) collective-permute-start(bf16[128,1024]{1,0:T(8,128)(2,1)} %get-tuple-element.111), channel_id=1, source_target_pairs={{0,3},{1,2},{2,1},{3,0},{4,7},{5,6},{6,5},{7,4},{8,11},{9,10},{10,... | collective-permute-start | bytes 786440 | tf_op jit(solution)/shard_map/ppermute | solution.py:368
  127.3 25.7 %collective-permute-start.51 = (bf16[128,1024]{1,0:T(8,128)(2,1)}, bf16[128,1024]{1,0:T(8,128)(2,1)}, u32[]{:S(2)}, u32[]{:S(2)}) collective-permute-start(bf16[128,1024]{1,0:T(8,128)(2,1)} %get-tuple-element.112), channel_id=1, source_target_pairs={{0,1},{1,0},{2,3},{3,2},{4,5},{5,4},{6,7},{7,6},{8,9},{9,8},{10,11... | collective-permute-start | bytes 786440 | tf_op jit(solution)/shard_map/ppermute | solution.py:368
  127.7 26.0 %collective-permute-start.50 = (bf16[128,1024]{1,0:T(8,128)(2,1)}, bf16[128,1024]{1,0:T(8,128)(2,1)}, u32[]{:S(2)}, u32[]{:S(2)}) collective-permute-start(bf16[128,1024]{1,0:T(8,128)(2,1)} %get-tuple-element.113), channel_id=1, source_target_pairs={{0,2},{1,3},{2,0},{3,1},{4,6},{5,7},{6,4},{7,5},{8,10},{9,11},{10,... | collective-permute-start | bytes 786440 | tf_op jit(solution)/shard_map/ppermute | solution.py:368
  129.0 25.2 %collective-permute-start.49 = (bf16[128,1024]{1,0:T(8,128)(2,1)}, bf16[128,1024]{1,0:T(8,128)(2,1)}, u32[]{:S(2)}, u32[]{:S(2)}) collective-permute-start(bf16[128,1024]{1,0:T(8,128)(2,1)} %collective-permute-done.47), channel_id=1, source_target_pairs={{0,1},{1,0},{2,3},{3,2},{4,5},{5,4},{6,7},{7,6},{8,9},{9,8},{10,11... | collective-permute-start | bytes 786440 | tf_op jit(solution)/shard_map/ppermute | solution.py:368
  146.1 71.0 %all-to-all-start.4 = ((bf16[8,384,128]{2,1,0:T(8,128)(2,1)}), bf16[8,384,128]{2,1,0:T(8,128)(2,1)}, u32[]{:S(2)}, u32[]{:S(2)}) async-start(bf16[8,384,128]{2,1,0:T(8,128)(2,1)} %attend_backward.1), calls=%async_computation.4 | async-start | bytes 1572864 | tf_op jit(solution)/shard_map/all_to_all | solution.py:356
  151.5 10.6 %collective-permute-start.13 = (bf16[128,1024]{0,1:T(8,128)(2,1)S(1)}, bf16[128,1024]{0,1:T(8,128)(2,1)S(1)}, u32[]{:S(2)}, u32[]{:S(2)}) collective-permute-start(bf16[128,1024]{0,1:T(8,128)(2,1)S(1)} %bitcast.283), channel_id=1, source_target_pairs={{0,2},{1,3},{2,0},{3,1},{4,6},{5,7},{6,4},{7,5},{8,10},{9,11},{10,... | collective-permute-start | bytes 786440 | tf_op jit(solution)/shard_map/ppermute | solution.py:368
  152.2 17.6 %collective-permute-start.14 = (bf16[128,1024]{0,1:T(8,128)(2,1)S(1)}, bf16[128,1024]{0,1:T(8,128)(2,1)S(1)}, u32[]{:S(2)}, u32[]{:S(2)}) collective-permute-start(bf16[128,1024]{0,1:T(8,128)(2,1)S(1)} %bitcast.284), channel_id=1, source_target_pairs={{0,1},{1,0},{2,3},{3,2},{4,5},{5,4},{6,7},{7,6},{8,9},{9,8},{10,11... | collective-permute-start | bytes 786440 | tf_op jit(solution)/shard_map/ppermute | solution.py:368
  154.2 31.0 %collective-permute-start.69 = (bf16[4,128,1024]{2,1,0:T(8,128)(2,1)}, bf16[4,128,1024]{2,1,0:T(8,128)(2,1)S(1)}, u32[]{:S(2)}, u32[]{:S(2)}) collective-permute-start(bf16[4,128,1024]{2,1,0:T(8,128)(2,1)} %fusion.19), channel_id=1, source_target_pairs={{0,4},{4,0},{8,12},{12,8},{16,20},{20,16},{24,28},{28,24},{1,5},{5... | collective-permute-start | bytes 3145736 | tf_op jit(solution)/shard_map/ppermute | solution.py:368
  162.1 45.6 %collective-permute-start.53 = (bf16[4,128,1024]{2,1,0:T(8,128)(2,1)S(1)}, bf16[4,128,1024]{2,1,0:T(8,128)(2,1)S(1)}, u32[]{:S(2)}, u32[]{:S(2)}) collective-permute-start(bf16[4,128,1024]{2,1,0:T(8,128)(2,1)S(1)} %fusion.18), channel_id=1, source_target_pairs={{0,4},{4,0},{8,12},{12,8},{16,20},{20,16},{24,28},{28,24},{1,5},{5... | collective-permute-start | bytes 3145736 | tf_op jit(solution)/shard_map/ppermute | solution.py:368
  169.0 88.1 %collective-permute-start.25 = (bf16[128,1024]{1,0:T(8,128)(2,1)}, bf16[128,1024]{1,0:T(8,128)(2,1)}, u32[]{:S(2)}, u32[]{:S(2)}) collective-permute-start(bf16[128,1024]{1,0:T(8,128)(2,1)} %multiply_convert_fusion.3), channel_id=1, source_target_pairs={{0,2},{1,3},{2,0},{3,1},{4,6},{5,7},{6,4},{7,5},{8,10},{9,11},{10,... | collective-permute-start | bytes 786440 | tf_op jit(solution)/shard_map/ppermute | solution.py:368
  169.8 78.8 %collective-permute-start.19 = (bf16[128,1024]{1,0:T(8,128)(2,1)}, bf16[128,1024]{1,0:T(8,128)(2,1)}, u32[]{:S(2)}, u32[]{:S(2)}) collective-permute-start(bf16[128,1024]{1,0:T(8,128)(2,1)} %get-tuple-element.25), channel_id=1, source_target_pairs={{0,2},{1,3},{2,0},{3,1},{4,6},{5,7},{6,4},{7,5},{8,10},{9,11},{10,... | collective-permute-start | bytes 786440 | tf_op jit(solution)/shard_map/ppermute | solution.py:368
  186.6 27.6 %collective-permute-start.70 = (bf16[128,1024]{1,0:T(8,128)(2,1)S(1)}, bf16[128,1024]{1,0:T(8,128)(2,1)S(1)}, u32[]{:S(2)}, u32[]{:S(2)}) collective-permute-start(bf16[128,1024]{1,0:T(8,128)(2,1)S(1)} %get-tuple-element.60), channel_id=1, source_target_pairs={{0,8},{4,12},{1,9},{5,13},{2,10},{6,14},{3,11},{7,15}} | collective-permute-start | bytes 786440 | tf_op jit(solution)/shard_map/ppermute | solution.py:364
  189.7 61.4 %collective-permute-start.73 = (bf16[128,1024]{1,0:T(8,128)(2,1)}, bf16[128,1024]{1,0:T(8,128)(2,1)}, u32[]{:S(2)}, u32[]{:S(2)}) collective-permute-start(bf16[128,1024]{1,0:T(8,128)(2,1)} %get-tuple-element.61), channel_id=1, source_target_pairs={{24,16},{28,20},{25,17},{29,21},{26,18},{30,22},{27,19},{31,23}} | collective-permute-start | bytes 786440 | tf_op jit(solution)/shard_map/ppermute | solution.py:364
  210.3 38.4 %collective-permute-start.54 = (bf16[128,1024]{1,0:T(8,128)(2,1)}, bf16[128,1024]{1,0:T(8,128)(2,1)}, u32[]{:S(2)}, u32[]{:S(2)}) collective-permute-start(bf16[128,1024]{1,0:T(8,128)(2,1)} %get-tuple-element.64), channel_id=1, source_target_pairs={{0,8},{4,12},{1,9},{5,13},{2,10},{6,14},{3,11},{7,15}} | collective-permute-start | bytes 786440 | tf_op jit(solution)/shard_map/ppermute | solution.py:364
  214.9 36.3 %collective-permute-start.71 = (bf16[128,1024]{1,0:T(8,128)(2,1)}, bf16[128,1024]{1,0:T(8,128)(2,1)}, u32[]{:S(2)}, u32[]{:S(2)}) collective-permute-start(bf16[128,1024]{1,0:T(8,128)(2,1)} %fusion.91), channel_id=1, source_target_pairs={{0,8},{4,12},{8,16},{12,20},{1,9},{5,13},{9,17},{13,21},{2,10},{6,... | collective-permute-start | bytes 786440 | tf_op jit(solution)/shard_map/ppermute | solution.py:364
  243.9 20.4 %all-to-all-start.5 = ((bf16[4,2,12288]{2,1,0:T(2,128)(2,1)}), bf16[4,2,12288]{2,1,0:T(2,128)(2,1)}, u32[]{:S(2)}, u32[]{:S(2)}) async-start(bf16[4,2,12288]{2,1,0:T(2,128)(2,1)} %reshape.313), calls=%async_computation.5 | async-start | bytes 393216 | tf_op jit(solution)/shard_map/all_to_all | solution.py:572
  248.6 8.8 %collective-permute-start.20 = (bf16[128,1024]{1,0:T(8,128)(2,1)}, bf16[128,1024]{1,0:T(8,128)(2,1)S(1)}, u32[]{:S(2)}, u32[]{:S(2)}) collective-permute-start(bf16[128,1024]{1,0:T(8,128)(2,1)} %get-tuple-element.25), channel_id=1, source_target_pairs={{0,1},{1,0},{2,3},{3,2},{4,5},{5,4},{6,7},{7,6},{8,9},{9,8},{10,11... | collective-permute-start | bytes 786440 | tf_op jit(solution)/shard_map/ppermute | solution.py:368
  248.8 9.7 %collective-permute-start.21 = (bf16[128,1024]{1,0:T(8,128)(2,1)}, bf16[128,1024]{1,0:T(8,128)(2,1)S(1)}, u32[]{:S(2)}, u32[]{:S(2)}) collective-permute-start(bf16[128,1024]{1,0:T(8,128)(2,1)} %collective-permute-done.19), channel_id=1, source_target_pairs={{0,1},{1,0},{2,3},{3,2},{4,5},{5,4},{6,7},{7,6},{8,9},{9,8},{10,11... | collective-permute-start | bytes 786440 | tf_op jit(solution)/shard_map/ppermute | solution.py:368
  251.0 12.5 %collective-permute-start.8 = (f32[17,2048]{1,0:T(8,128)}, f32[17,2048]{1,0:T(8,128)S(1)}, u32[]{:S(2)}, u32[]{:S(2)}) collective-permute-start(f32[17,2048]{1,0:T(8,128)} %fusion.125), channel_id=1, source_target_pairs={{0,1},{1,0},{2,3},{3,2},{4,5},{5,4},{6,7},{7,6},{8,9},{9,8},{10,11... | collective-permute-start | bytes 417800 | tf_op jit(solution)/shard_map/ppermute | solution.py:368
  258.9 9.1 %collective-permute-start.27 = (bf16[128,1024]{1,0:T(8,128)(2,1)}, bf16[128,1024]{1,0:T(8,128)(2,1)}, u32[]{:S(2)}, u32[]{:S(2)}) collective-permute-start(bf16[128,1024]{1,0:T(8,128)(2,1)} %collective-permute-done.25), channel_id=1, source_target_pairs={{0,1},{1,0},{2,3},{3,2},{4,5},{5,4},{6,7},{7,6},{8,9},{9,8},{10,11... | collective-permute-start | bytes 786440 | tf_op jit(solution)/shard_map/ppermute | solution.py:368
  259.0 9.3 %collective-permute-start.30 = (bf16[128,768]{0,1:T(8,128)(2,1)}, bf16[128,768]{0,1:T(8,128)(2,1)}, u32[]{:S(2)}, u32[]{:S(2)}) collective-permute-start(bf16[128,768]{0,1:T(8,128)(2,1)} %get-tuple-element.119), channel_id=1, source_target_pairs={{0,3},{1,2},{2,1},{3,0},{4,7},{5,6},{6,5},{7,4},{8,11},{9,10},{10,... | collective-permute-start | bytes 589832 | tf_op jit(solution)/shard_map/ppermute | solution.py:368
  261.0 9.7 %collective-permute-start.29 = (bf16[128,768]{0,1:T(8,128)(2,1)}, bf16[128,768]{0,1:T(8,128)(2,1)}, u32[]{:S(2)}, u32[]{:S(2)}) collective-permute-start(bf16[128,768]{0,1:T(8,128)(2,1)} %get-tuple-element.120), channel_id=1, source_target_pairs={{0,1},{1,0},{2,3},{3,2},{4,5},{5,4},{6,7},{7,6},{8,9},{9,8},{10,11... | collective-permute-start | bytes 589832 | tf_op jit(solution)/shard_map/ppermute | solution.py:368
  263.5 8.6 %collective-permute-start.28 = (bf16[128,768]{0,1:T(8,128)(2,1)}, bf16[128,768]{0,1:T(8,128)(2,1)}, u32[]{:S(2)}, u32[]{:S(2)}) collective-permute-start(bf16[128,768]{0,1:T(8,128)(2,1)} %get-tuple-element.121), channel_id=1, source_target_pairs={{0,2},{1,3},{2,0},{3,1},{4,6},{5,7},{6,4},{7,5},{8,10},{9,11},{10,... | collective-permute-start | bytes 589832 | tf_op jit(solution)/shard_map/ppermute | solution.py:368
  266.6 28.3 %collective-permute-start.57 = (bf16[128,1024]{1,0:T(8,128)(2,1)}, bf16[128,1024]{1,0:T(8,128)(2,1)}, u32[]{:S(2)}, u32[]{:S(2)}) collective-permute-start(bf16[128,1024]{1,0:T(8,128)(2,1)} %get-tuple-element.65), channel_id=1, source_target_pairs={{24,16},{28,20},{25,17},{29,21},{26,18},{30,22},{27,19},{31,23}} | collective-permute-start | bytes 786440 | tf_op jit(solution)/shard_map/ppermute | solution.py:364
  268.0 92.9 %collective-permute-start = (bf16[816,512]{1,0:T(8,128)(2,1)}, bf16[816,512]{1,0:T(8,128)(2,1)}, u32[]{:S(2)}, u32[]{:S(2)}) collective-permute-start(bf16[816,512]{1,0:T(8,128)(2,1)} %constant_dynamic-slice_fusion.27), channel_id=1, source_target_pairs={{0,1},{1,0},{2,3},{3,2},{4,5},{5,4},{6,7},{7,6},{8,9},{9,8},{10,11... | collective-permute-start | bytes 2506760 | tf_op jit(solution)/shard_map/ppermute | solution.py:368
  268.3 28.1 %collective-permute-start.55 = (bf16[128,1024]{1,0:T(8,128)(2,1)}, bf16[128,1024]{1,0:T(8,128)(2,1)}, u32[]{:S(2)}, u32[]{:S(2)}) collective-permute-start(bf16[128,1024]{1,0:T(8,128)(2,1)} %fusion.97), channel_id=1, source_target_pairs={{0,8},{4,12},{8,16},{12,20},{1,9},{5,13},{9,17},{13,21},{2,10},{6,... | collective-permute-start | bytes 786440 | tf_op jit(solution)/shard_map/ppermute | solution.py:364
  270.8 29.3 %collective-permute-start.74 = (bf16[128,1024]{1,0:T(8,128)(2,1)}, bf16[128,1024]{1,0:T(8,128)(2,1)}, u32[]{:S(2)}, u32[]{:S(2)}) collective-permute-start(bf16[128,1024]{1,0:T(8,128)(2,1)} %get-tuple-element.59), channel_id=1, source_target_pairs={{16,8},{20,12},{24,16},{28,20},{17,9},{21,13},{25,17},{29,21},{18,... | collective-permute-start | bytes 786440 | tf_op jit(solution)/shard_map/ppermute | solution.py:364
  272.1 58.6 %collective-permute-start.72 = (bf16[128,1024]{1,0:T(8,128)(2,1)}, bf16[128,1024]{1,0:T(8,128)(2,1)}, u32[]{:S(2)}, u32[]{:S(2)}) collective-permute-start(bf16[128,1024]{1,0:T(8,128)(2,1)} %get-tuple-element.58), channel_id=1, source_target_pairs={{0,8},{4,12},{8,16},{12,20},{16,24},{20,28},{1,9},{5,13},{9,17},{1... | collective-permute-start | bytes 786440 | tf_op jit(solution)/shard_map/ppermute | solution.py:364
  298.7 23.1 %collective-permute-start.58 = (bf16[128,1024]{1,0:T(8,128)(2,1)}, bf16[128,1024]{1,0:T(8,128)(2,1)}, u32[]{:S(2)}, u32[]{:S(2)}) collective-permute-start(bf16[128,1024]{1,0:T(8,128)(2,1)} %get-tuple-element.63), channel_id=1, source_target_pairs={{16,8},{20,12},{24,16},{28,20},{17,9},{21,13},{25,17},{29,21},{18,... | collective-permute-start | bytes 786440 | tf_op jit(solution)/shard_map/ppermute | solution.py:364
  302.0 30.2 %collective-permute-start.75 = (bf16[128,1024]{1,0:T(8,128)(2,1)}, bf16[128,1024]{1,0:T(8,128)(2,1)}, u32[]{:S(2)}, u32[]{:S(2)}) collective-permute-start(bf16[128,1024]{1,0:T(8,128)(2,1)} %fusion.90), channel_id=1, source_target_pairs={{8,0},{12,4},{16,8},{20,12},{24,16},{28,20},{9,1},{13,5},{17,9},{2... | collective-permute-start | bytes 786440 | tf_op jit(solution)/shard_map/ppermute | solution.py:364
  304.0 15.5 %collective-permute-start.10 = (f32[17,2048]{1,0:T(8,128)}, f32[17,2048]{1,0:T(8,128)}, u32[]{:S(2)}, u32[]{:S(2)}) collective-permute-start(f32[17,2048]{1,0:T(8,128)} %add.566), channel_id=1, source_target_pairs={{0,4},{4,0},{8,12},{12,8},{16,20},{20,16},{24,28},{28,24},{1,5},{5... | collective-permute-start | bytes 417800 | tf_op jit(solution)/shard_map/ppermute | solution.py:368
  319.5 43.6 %collective-permute-start.31 = (bf16[4,128,1280]{2,1,0:T(8,128)(2,1)S(1)}, bf16[4,128,1280]{2,1,0:T(8,128)(2,1)S(1)}, u32[]{:S(2)}, u32[]{:S(2)}) collective-permute-start(bf16[4,128,1280]{2,1,0:T(8,128)(2,1)S(1)} %bitcast.281), channel_id=1, source_target_pairs={{0,4},{4,0},{8,12},{12,8},{16,20},{20,16},{24,28},{28,24},{1,5},{5... | collective-permute-start | bytes 3932168 | tf_op jit(solution)/shard_map/ppermute | solution.py:368
  327.5 23.8 %collective-permute-start.56 = (bf16[128,1024]{1,0:T(8,128)(2,1)}, bf16[128,1024]{1,0:T(8,128)(2,1)S(1)}, u32[]{:S(2)}, u32[]{:S(2)}) collective-permute-start(bf16[128,1024]{1,0:T(8,128)(2,1)} %get-tuple-element.62), channel_id=1, source_target_pairs={{0,8},{4,12},{8,16},{12,20},{16,24},{20,28},{1,9},{5,13},{9,17},{1... | collective-permute-start | bytes 786440 | tf_op jit(solution)/shard_map/ppermute | solution.py:364
  330.7 27.2 %collective-permute-start.59 = (bf16[128,1024]{1,0:T(8,128)(2,1)S(1)}, bf16[128,1024]{1,0:T(8,128)(2,1)S(1)}, u32[]{:S(2)}, u32[]{:S(2)}) collective-permute-start(bf16[128,1024]{1,0:T(8,128)(2,1)S(1)} %fusion.96), channel_id=1, source_target_pairs={{8,0},{12,4},{16,8},{20,12},{24,16},{28,20},{9,1},{13,5},{17,9},{2... | collective-permute-start | bytes 786440 | tf_op jit(solution)/shard_map/ppermute | solution.py:364
  332.1 13.7 %collective-permute-start.12 = (f32[17,2048]{1,0:T(8,128)S(1)}, f32[17,2048]{1,0:T(8,128)S(1)}, u32[]{:S(2)}, u32[]{:S(2)}) collective-permute-start(f32[17,2048]{1,0:T(8,128)S(1)} %add.568), channel_id=1, source_target_pairs={{0,16},{4,20},{8,24},{12,28},{16,0},{20,4},{24,8},{28,12},{1,17},{... | collective-permute-start | bytes 417800 | tf_op jit(solution)/shard_map/ppermute | solution.py:368
  345.8 14.8 %collective-permute-start.77 = (bf16[128,1024]{1,0:T(8,128)(2,1)S(1)}, bf16[128,1024]{1,0:T(8,128)(2,1)S(1)}, u32[]{:S(2)}, u32[]{:S(2)}) collective-permute-start(bf16[128,1024]{1,0:T(8,128)(2,1)S(1)} %fusion.94), channel_id=1, source_target_pairs={{0,2},{1,3},{2,0},{3,1},{4,6},{5,7},{6,4},{7,5},{8,10},{9,11},{10,... | collective-permute-start | bytes 786440 | tf_op jit(solution)/shard_map/ppermute | solution.py:368
  351.3 11.3 %collective-permute-start.76 = (bf16[128,1024]{1,0:T(8,128)(2,1)S(1)}, bf16[128,1024]{1,0:T(8,128)(2,1)S(1)}, u32[]{:S(2)}, u32[]{:S(2)}) collective-permute-start(bf16[128,1024]{1,0:T(8,128)(2,1)S(1)} %fusion.94), channel_id=1, source_target_pairs={{0,1},{1,0},{2,3},{3,2},{4,5},{5,4},{6,7},{7,6},{8,9},{9,8},{10,11... | collective-permute-start | bytes 786440 | tf_op jit(solution)/shard_map/ppermute | solution.py:368
  359.1 21.2 %collective-permute-start.61 = (bf16[128,1024]{1,0:T(8,128)(2,1)S(1)}, bf16[128,1024]{1,0:T(8,128)(2,1)S(1)}, u32[]{:S(2)}, u32[]{:S(2)}) collective-permute-start(bf16[128,1024]{1,0:T(8,128)(2,1)S(1)} %fusion.100), channel_id=1, source_target_pairs={{0,2},{1,3},{2,0},{3,1},{4,6},{5,7},{6,4},{7,5},{8,10},{9,11},{10,... | collective-permute-start | bytes 786440 | tf_op jit(solution)/shard_map/ppermute | solution.py:368
  360.6 27.1 %collective-permute-start.60 = (bf16[128,1024]{1,0:T(8,128)(2,1)S(1)}, bf16[128,1024]{1,0:T(8,128)(2,1)S(1)}, u32[]{:S(2)}, u32[]{:S(2)}) collective-permute-start(bf16[128,1024]{1,0:T(8,128)(2,1)S(1)} %fusion.100), channel_id=1, source_target_pairs={{0,1},{1,0},{2,3},{3,2},{4,5},{5,4},{6,7},{7,6},{8,9},{9,8},{10,11... | collective-permute-start | bytes 786440 | tf_op jit(solution)/shard_map/ppermute | solution.py:368
  362.7 13.4 %collective-permute-start.1 = (bf16[816,256]{1,0:T(8,128)(2,1)S(1)}, bf16[816,256]{1,0:T(8,128)(2,1)S(1)}, u32[]{:S(2)}, u32[]{:S(2)}) collective-permute-start(bf16[816,256]{1,0:T(8,128)(2,1)S(1)} %dynamic-slice_convert_fusion.2), channel_id=1, source_target_pairs={{0,2},{1,3},{2,0},{3,1},{4,6},{5,7},{6,4},{7,5},{8,10},{9,11},{10,... | collective-permute-start | bytes 1253384 | tf_op jit(solution)/shard_map/ppermute | solution.py:368
  364.9 12.3 %collective-permute-start.32 = (bf16[128,1280]{1,0:T(8,128)(2,1)S(1)}, bf16[128,1280]{1,0:T(8,128)(2,1)S(1)}, u32[]{:S(2)}, u32[]{:S(2)}) collective-permute-start(bf16[128,1280]{1,0:T(8,128)(2,1)S(1)} %get-tuple-element.56), channel_id=1, source_target_pairs={{0,8},{4,12},{1,9},{5,13},{2,10},{6,14},{3,11},{7,15}} | collective-permute-start | bytes 983048 | tf_op jit(solution)/shard_map/ppermute | solution.py:364
  376.2 10.4 %collective-permute-start.2 = (bf16[816,256]{1,0:T(8,128)(2,1)S(1)}, bf16[816,256]{1,0:T(8,128)(2,1)S(1)}, u32[]{:S(2)}, u32[]{:S(2)}) collective-permute-start(bf16[816,256]{1,0:T(8,128)(2,1)S(1)} %add_convert_fusion.4), channel_id=1, source_target_pairs={{0,4},{4,0},{8,12},{12,8},{16,20},{20,16},{24,28},{28,24},{1,5},{5... | collective-permute-start | bytes 1253384 | tf_op jit(solution)/shard_map/ppermute | solution.py:368
  376.5 10.3 %collective-permute-start.35 = (bf16[128,1280]{1,0:T(8,128)(2,1)S(1)}, bf16[128,1280]{1,0:T(8,128)(2,1)S(1)}, u32[]{:S(2)}, u32[]{:S(2)}) collective-permute-start(bf16[128,1280]{1,0:T(8,128)(2,1)S(1)} %get-tuple-element.57), channel_id=1, source_target_pairs={{24,16},{28,20},{25,17},{29,21},{26,18},{30,22},{27,19},{31,23}} | collective-permute-start | bytes 983048 | tf_op jit(solution)/shard_map/ppermute | solution.py:364
  377.3 9.5 %collective-permute-start.33 = (bf16[128,1280]{1,0:T(8,128)(2,1)S(1)}, bf16[128,1280]{1,0:T(8,128)(2,1)S(1)}, u32[]{:S(2)}, u32[]{:S(2)}) collective-permute-start(bf16[128,1280]{1,0:T(8,128)(2,1)S(1)} %fusion.83), channel_id=1, source_target_pairs={{0,8},{4,12},{8,16},{12,20},{1,9},{5,13},{9,17},{13,21},{2,10},{6,... | collective-permute-start | bytes 983048 | tf_op jit(solution)/shard_map/ppermute | solution.py:364
  386.8 9.5 %collective-permute-start.3 = (bf16[816,256]{1,0:T(8,128)(2,1)S(1)}, bf16[816,256]{1,0:T(8,128)(2,1)S(1)}, u32[]{:S(2)}, u32[]{:S(2)}) collective-permute-start(bf16[816,256]{1,0:T(8,128)(2,1)S(1)} %add_convert_fusion.3), channel_id=1, source_target_pairs={{0,8},{4,12},{8,0},{12,4},{16,24},{20,28},{24,16},{28,20},{1,9},{5... | collective-permute-start | bytes 1253384 | tf_op jit(solution)/shard_map/ppermute | solution.py:368
  387.0 11.7 %collective-permute-start.36 = (bf16[128,1280]{1,0:T(8,128)(2,1)S(1)}, bf16[128,1280]{1,0:T(8,128)(2,1)S(1)}, u32[]{:S(2)}, u32[]{:S(2)}) collective-permute-start(bf16[128,1280]{1,0:T(8,128)(2,1)S(1)} %get-tuple-element.55), channel_id=1, source_target_pairs={{16,8},{20,12},{24,16},{28,20},{17,9},{21,13},{25,17},{29,21},{18,... | collective-permute-start | bytes 983048 | tf_op jit(solution)/shard_map/ppermute | solution.py:364
  396.4 18.5 %collective-permute-start.4 = (bf16[816,256]{1,0:T(8,128)(2,1)S(1)}, bf16[816,256]{1,0:T(8,128)(2,1)S(1)}, u32[]{:S(2)}, u32[]{:S(2)}) collective-permute-start(bf16[816,256]{1,0:T(8,128)(2,1)S(1)} %add_convert_fusion.2), channel_id=1, source_target_pairs={{0,16},{4,20},{8,24},{12,28},{16,0},{20,4},{24,8},{28,12},{1,17},{... | collective-permute-start | bytes 1253384 | tf_op jit(solution)/shard_map/ppermute | solution.py:368
  396.5 20.1 %collective-permute-start.34 = (bf16[128,1280]{1,0:T(8,128)(2,1)S(1)}, bf16[128,1280]{1,0:T(8,128)(2,1)S(1)}, u32[]{:S(2)}, u32[]{:S(2)}) collective-permute-start(bf16[128,1280]{1,0:T(8,128)(2,1)S(1)} %get-tuple-element.54), channel_id=1, source_target_pairs={{0,8},{4,12},{8,16},{12,20},{16,24},{20,28},{1,9},{5,13},{9,17},{1... | collective-permute-start | bytes 983048 | tf_op jit(solution)/shard_map/ppermute | solution.py:364
  398.8 17.8 %collective-permute-start.37 = (bf16[128,1280]{1,0:T(8,128)(2,1)S(1)}, bf16[128,1280]{1,0:T(8,128)(2,1)S(1)}, u32[]{:S(2)}, u32[]{:S(2)}) collective-permute-start(bf16[128,1280]{1,0:T(8,128)(2,1)S(1)} %fusion.82), channel_id=1, source_target_pairs={{8,0},{12,4},{16,8},{20,12},{24,16},{28,20},{9,1},{13,5},{17,9},{2... | collective-permute-start | bytes 983048 | tf_op jit(solution)/shard_map/ppermute | solution.py:364
  415.0 18.3 %collective-permute-start.6 = (bf16[816,256]{1,0:T(8,128)(2,1)S(1)}, bf16[816,256]{1,0:T(8,128)(2,1)S(1)}, u32[]{:S(2)}, u32[]{:S(2)}) collective-permute-start(bf16[816,256]{1,0:T(8,128)(2,1)S(1)} %add_convert_fusion.1), channel_id=1, source_target_pairs={{0,2},{1,3},{2,0},{3,1},{4,6},{5,7},{6,4},{7,5},{8,10},{9,11},{10,... | collective-permute-start | bytes 1253384 | tf_op jit(solution)/shard_map/ppermute | solution.py:368
  416.7 9.8 %collective-permute-start.45 = (bf16[128,256]{1,0:T(8,128)(2,1)S(1)}, bf16[128,256]{1,0:T(8,128)(2,1)S(1)}, u32[]{:S(2)}, u32[]{:S(2)}) collective-permute-start(bf16[128,256]{1,0:T(8,128)(2,1)S(1)} %get-tuple-element.124), channel_id=1, source_target_pairs={{0,2},{1,3},{2,0},{3,1},{4,6},{5,7},{6,4},{7,5},{8,10},{9,11},{10,... | collective-permute-start | bytes 196616 | tf_op jit(solution)/shard_map/ppermute | solution.py:368
  418.4 23.0 %collective-permute-start.5 = (bf16[816,256]{1,0:T(8,128)(2,1)S(1)}, bf16[816,256]{1,0:T(8,128)(2,1)S(1)}, u32[]{:S(2)}, u32[]{:S(2)}) collective-permute-start(bf16[816,256]{1,0:T(8,128)(2,1)S(1)} %add_convert_fusion.1), channel_id=1, source_target_pairs={{0,1},{1,0},{2,3},{3,2},{4,5},{5,4},{6,7},{7,6},{8,9},{9,8},{10,11... | collective-permute-start | bytes 1253384 | tf_op jit(solution)/shard_map/ppermute | solution.py:368
  (71 other events, 496.0 us)
